TPU v7x, 32 devices: a whole 2x2x4 slice. The times are simulated.
32 devices in a mesh: dp: 2 (over core), expert: 4 (over z), tensor: 4 (over y, x).
Axes of the slice: x: 2, y: 2, z: 4, core: 2. Of those that a mesh axis runs over, the one named last changes fastest.
Arguments:
- tokens: bfloat16 [24, 197, 768], P(('dp', 'expert'))
- cotangent: bfloat16 [24, 197, 768], P(('dp', 'expert')), may hold values from -6 to 6
- expert_ids: int32 [24, 197, 2], P(('dp', 'expert')), may hold values from 0 to 3, as said below
- slot_rank: int32 [24, 197, 2], P(('dp', 'expert')), may hold values from -1 to 368, as said below
- qkv_weight: bfloat16 [3, 768, 768], P(None, None, 'tensor'), may hold values from -0.3125 to 0.3125
- out_weight: bfloat16 [768, 768], P('tensor'), may hold values from -0.625 to 0.625
- router_weight: bfloat16 [768, 4], replicated, may hold values from -0.15625 to 0.15625
- expert_in: bfloat16 [4, 768, 3072], P('expert', None, 'tensor'), may hold values from -0.21875 to 0.21875
- expert_out: bfloat16 [4, 3072, 768], P('expert', 'tensor'), may hold values from -0.875 to 0.875
- gain_attention: float32 [768], replicated, may hold values from 0.25 to 1.75
- gain_experts: float32 [768], replicated, may hold values from 0.25 to 1.75
Outputs:
- block_out: bfloat16 [24, 197, 768], P(('dp', 'expert'))
- grad_tokens: float32 [24, 197, 768], P(('dp', 'expert'))
- grad_qkv: float32 [3, 768, 768], P(None, None, 'tensor')
- grad_out: float32 [768, 768], P('tensor')
- grad_router: float32 [768, 4], replicated
- grad_expert_in: float32 [4, 768, 3072], P('expert', None, 'tensor')
- grad_expert_out: float32 [4, 3072, 768], P('expert', 'tensor')
- grad_gain_attention: float32 [768], replicated
- grad_gain_experts: float32 [768], replicated
- balance_loss: float32 [], replicated
Inputs may be any that keep to these rules, and one draw needn't show every extreme that they name: `expert_ids`: the two experts of a token differ. Within each aligned block of 591 tokens, the pairs that name one expert are ranked: first choices of all the block's tokens in token order, then second choices in token order. A pair's slot_rank is its rank if that is below 369, else -1. In every block some expert has its slot 368 filled and a pair dropped.
All inputs are finite; a program needn't handle non-finite values.
Results may differ from a plain program's by a relative error of at most 0.017.
The roundings to bfloat16 on the way count: a program that leaves them out, or rounds other values in their place, can miss the bound.
Values may be sent and summed in bfloat16 or wider, within the bound.
No kernel may reach another device: no remote copies, remote signals or barrier semaphores. Data moves between devices by JAX's collectives and lax.ppermute only.
A program may use at most 192 MiB of HBM per device.

v0:
```python
import jax
import jax.numpy as jnp
from jax import lax
from jax.sharding import PartitionSpec as P

HD = 64


epsilon = 1e-06


def normalize(values, gain_row):
    center = values - jnp.mean(values, axis=-1, keepdims=True)
    inverse = lax.rsqrt(jnp.mean(center * center, axis=-1, keepdims=True) + epsilon)
    normed = center * inverse
    return (normed, inverse, normed * gain_row)


def normalize_back(upstream, normed, inverse, gain_row):
    scaled = upstream * gain_row
    result = inverse * (
        scaled
        - jnp.mean(scaled, axis=-1, keepdims=True)
        - normed * jnp.mean(scaled * normed, axis=-1, keepdims=True)
    )
    return (result, jnp.sum(upstream * normed, axis=0))


def exact_gelu(values):
    return jax.nn.gelu(values, approximate=False)


def body(
    tokens,
    cotangent,
    expert_ids,
    slot_rank,
    qkv_weight,
    out_weight,
    router_weight,
    expert_in,
    expert_out,
    gain_attention,
    gain_experts,
):
    images, seq_len, model_width = tokens.shape
    token_rows = images * seq_len
    local_width = qkv_weight.shape[2]
    local_heads = local_width // HD
    slice_width = model_width // lax.axis_size("tensor")
    experts = router_weight.shape[1]
    capacity = 5 * token_rows // (2 * experts)
    owners = lax.axis_size("expert")
    per_owner = experts // owners
    slot_total = experts * capacity
    score_scale = HD ** (-0.5)
    inputs = tokens.reshape(token_rows, model_width).astype(jnp.float32)
    normed_one, inverse_one, mixed_one = normalize(inputs, gain_attention)
    entered = mixed_one.astype(jnp.bfloat16)
    project = jnp.einsum(
        "td,cdf->ctf", entered, qkv_weight, preferred_element_type=jnp.float32
    ).astype(jnp.bfloat16)
    projected_heads = project.reshape(3, images, seq_len, local_heads, HD)
    queries, key_rows, value_rows = (projected_heads[0], projected_heads[1], projected_heads[2])
    scores = (
        jnp.einsum("ishe,ithe->ihst", queries, key_rows, preferred_element_type=jnp.float32)
        * score_scale
    )
    log_total = jax.nn.logsumexp(scores, axis=-1, keepdims=True)
    attn_probs = jnp.exp(scores - log_total).astype(jnp.bfloat16)
    attended = jnp.einsum(
        "ihst,ithe->ishe", attn_probs, value_rows, preferred_element_type=jnp.float32
    )
    attended = attended.astype(jnp.bfloat16).reshape(token_rows, local_width)
    attn_part = jnp.dot(attended, out_weight, preferred_element_type=jnp.float32)
    residual = inputs + lax.psum(attn_part, "tensor")
    normed_two, inverse_two, mixed_two = normalize(residual, gain_experts)
    routed = mixed_two.astype(jnp.bfloat16)
    route_prob = jax.nn.softmax(
        jnp.dot(routed, router_weight, preferred_element_type=jnp.float32), axis=-1
    )
    chosen = expert_ids.reshape(token_rows, 2)
    ranked = slot_rank.reshape(token_rows, 2)
    kept_mask = (ranked >= 0).astype(jnp.float32)
    position = jnp.where(ranked >= 0, chosen * capacity + ranked, slot_total).reshape(-1)
    send_rows = (
        jnp.zeros((slot_total, model_width), jnp.bfloat16)
        .at[position]
        .set(jnp.repeat(routed, 2, axis=0), mode="drop")
        .reshape(experts, capacity, model_width)
    )
    fragment = lax.all_to_all(send_rows, "expert", split_axis=0, concat_axis=0, tiled=True)
    grouped = fragment.reshape(owners, per_owner, fragment.shape[1], model_width)
    before = jnp.einsum("sjcd,jdf->sjcf", grouped, expert_in, preferred_element_type=jnp.float32)
    hidden = exact_gelu(before).astype(jnp.bfloat16)
    expert_part = jnp.einsum(
        "sjcf,jfd->sjcd", hidden, expert_out, preferred_element_type=jnp.float32
    )
    produced = lax.psum_scatter(expert_part, "tensor", scatter_dimension=3, tiled=True).astype(
        jnp.bfloat16
    )
    returned = lax.all_to_all(
        produced.reshape(experts, capacity, slice_width),
        "expert",
        split_axis=0,
        concat_axis=0,
        tiled=True,
    )
    returned = lax.all_gather(returned, "tensor", axis=2, tiled=True).reshape(
        slot_total, model_width
    )
    safe_index = jnp.minimum(position, slot_total - 1)
    picked = returned[safe_index].reshape(token_rows, 2, model_width).astype(jnp.float32)
    gate_values = jnp.take_along_axis(route_prob, chosen, axis=1) * kept_mask
    output = residual + jnp.sum(gate_values[:, :, None] * picked, axis=1)
    block_out = output.astype(jnp.bfloat16).reshape(images, seq_len, model_width)
    upstream = cotangent.reshape(token_rows, model_width).astype(jnp.float32)
    gate_grad = jnp.sum(upstream[:, None, :] * picked, axis=-1) * kept_mask
    member = (chosen[:, :, None] == jnp.arange(experts)[None, None, :]).astype(jnp.float32)
    route_grad = jnp.sum(member * gate_grad[:, :, None], axis=1)
    logit_grad = (
        route_prob * (route_grad - jnp.sum(route_grad * route_prob, axis=-1, keepdims=True))
    ).astype(jnp.bfloat16)
    row_grad = (
        (gate_values[:, :, None] * upstream[:, None, :])
        .astype(jnp.bfloat16)
        .reshape(2 * token_rows, model_width)
    )
    grad_send = (
        jnp.zeros((slot_total, model_width), jnp.bfloat16)
        .at[position]
        .set(row_grad, mode="drop")
        .reshape(experts, capacity, model_width)
    )
    grad_arrived = lax.all_to_all(grad_send, "expert", split_axis=0, concat_axis=0, tiled=True)
    grad_arrived = grad_arrived.reshape(owners, per_owner, capacity, model_width)
    hidden_grad = jnp.einsum(
        "sjcd,jfd->sjcf", grad_arrived, expert_out, preferred_element_type=jnp.float32
    )
    grad_expert_out = jnp.einsum(
        "sjcf,sjcd->jfd", hidden, grad_arrived, preferred_element_type=jnp.float32
    )
    pre_grad = jax.vjp(exact_gelu, before)[1](hidden_grad)[0].astype(jnp.bfloat16)
    grad_expert_in = jnp.einsum(
        "sjcd,sjcf->jdf", grouped, pre_grad, preferred_element_type=jnp.float32
    )
    buffer_part = jnp.einsum(
        "sjcf,jdf->sjcd", pre_grad, expert_in, preferred_element_type=jnp.float32
    )
    buffer_share = lax.psum_scatter(buffer_part, "tensor", scatter_dimension=3, tiled=True).astype(
        jnp.bfloat16
    )
    buffer_back = lax.all_to_all(
        buffer_share.reshape(experts, capacity, slice_width),
        "expert",
        split_axis=0,
        concat_axis=0,
        tiled=True,
    )
    buffer_grad = lax.all_gather(buffer_back, "tensor", axis=2, tiled=True).reshape(
        slot_total, model_width
    )
    routed_grad = jnp.sum(
        buffer_grad[safe_index].reshape(token_rows, 2, model_width).astype(jnp.float32)
        * kept_mask[:, :, None],
        axis=1,
    )
    routed_grad = routed_grad + jnp.dot(
        logit_grad, router_weight.T, preferred_element_type=jnp.float32
    )
    grad_router = jnp.einsum("td,te->de", routed, logit_grad, preferred_element_type=jnp.float32)
    from_norm_two, grad_gain_experts = normalize_back(
        routed_grad, normed_two, inverse_two, gain_experts
    )
    residual_grad = upstream + from_norm_two
    attn_grad = residual_grad.astype(jnp.bfloat16)
    grad_out = jnp.einsum("tf,td->fd", attended, attn_grad, preferred_element_type=jnp.float32)
    heads_grad = jnp.dot(attn_grad, out_weight.T, preferred_element_type=jnp.float32).astype(
        jnp.bfloat16
    )
    heads_grad = heads_grad.reshape(images, seq_len, local_heads, HD)
    again = (
        jnp.einsum("ishe,ithe->ihst", queries, key_rows, preferred_element_type=jnp.float32)
        * score_scale
    )
    probs_full = jnp.exp(again - log_total)
    prob_grad = jnp.einsum(
        "ishe,ithe->ihst", heads_grad, value_rows, preferred_element_type=jnp.float32
    )
    value_grad = jnp.einsum(
        "ihst,ishe->ithe",
        probs_full.astype(jnp.bfloat16),
        heads_grad,
        preferred_element_type=jnp.float32,
    )
    score_grad = (
        probs_full * (prob_grad - jnp.sum(prob_grad * probs_full, axis=-1, keepdims=True))
    ).astype(jnp.bfloat16)
    query_grad = (
        jnp.einsum("ihst,ithe->ishe", score_grad, key_rows, preferred_element_type=jnp.float32)
        * score_scale
    )
    key_grad = (
        jnp.einsum("ihst,ishe->ithe", score_grad, queries, preferred_element_type=jnp.float32)
        * score_scale
    )
    project_grad = (
        jnp.stack([query_grad, key_grad, value_grad])
        .astype(jnp.bfloat16)
        .reshape(3, token_rows, local_width)
    )
    grad_qkv = jnp.einsum("td,ctf->cdf", entered, project_grad, preferred_element_type=jnp.float32)
    entered_part = jnp.einsum(
        "ctf,cdf->td", project_grad, qkv_weight, preferred_element_type=jnp.float32
    )
    entered_grad = lax.psum(entered_part.astype(jnp.bfloat16), "tensor").astype(jnp.float32)
    from_norm_one, grad_gain_attention = normalize_back(
        entered_grad, normed_one, inverse_one, gain_attention
    )
    grad_tokens = (residual_grad + from_norm_one).reshape(images, seq_len, model_width)
    counts = jnp.sum(member, axis=(0, 1))
    prob_sum = jnp.sum(route_prob, axis=0)
    grad_qkv, grad_out, grad_router, grad_gain_attention, grad_gain_experts, counts, prob_sum = (
        lax.psum(
            (
                grad_qkv,
                grad_out,
                grad_router,
                grad_gain_attention,
                grad_gain_experts,
                counts,
                prob_sum,
            ),
            ("dp", "expert"),
        )
    )
    grad_expert_in, grad_expert_out = (
        lax.psum(grad_expert_in.astype(jnp.bfloat16), "dp").astype(jnp.float32),
        lax.psum(grad_expert_out.astype(jnp.bfloat16), "dp").astype(jnp.float32),
    )
    token_total = token_rows * lax.axis_size("dp") * lax.axis_size("expert")
    balance_loss = experts * jnp.sum(counts / (2.0 * token_total) * prob_sum / token_total)
    return (
        block_out,
        grad_tokens,
        grad_qkv,
        grad_out,
        grad_router,
        grad_expert_in,
        grad_expert_out,
        grad_gain_attention,
        grad_gain_experts,
        balance_loss,
    )


def solution(mesh):
    placed = (
        P(("dp", "expert"), None, None),
        P(("dp", "expert"), None, None),
        P(("dp", "expert"), None, None),
        P(("dp", "expert"), None, None),
        P(None, None, "tensor"),
        P("tensor", None),
        P(),
        P("expert", None, "tensor"),
        P("expert", "tensor", None),
        P(),
        P(),
    )
    return jax.shard_map(
        body,
        mesh=mesh,
        in_specs=placed,
        out_specs=(
            P(("dp", "expert"), None, None),
            P(("dp", "expert"), None, None),
            P(None, None, "tensor"),
            P("tensor", None),
            P(),
            P("expert", None, "tensor"),
            P("expert", "tensor", None),
            P(),
            P(),
            P(),
        ),
        check_vma=False,
    )
```

profile of v0, /device:TPU:0, one launch (start us, length us, event | category | flops | bytes accessed | tf_op | source)
XLA Modules:
  0.0 862.4 jit_solution(6967606850585133107)
XLA Ops:
  29.1 66.8 %all-reduce.12.cloned.1.call-done = f32[591,768]{1,0:T(8,128)} async-done(((f32[591,768]{1,0:T(8,128)}), f32[591,768]{1,0:T(8,128)}) %all-reduce.12.cloned.1.call-update) | async-done | bytes 1815568 | tf_op jit(solution)/shard_map/psum | solution.py:76
  105.7 9.6 %scatter_custom_fusion = bf16[1476,768]{1,0:T(8,128)(2,1)S(1)} fusion(s32[1182]{0:T(1024)S(1)} %get-tuple-element.23, bf16[1182,768]{1,0:T(8,128)(2,1)} %reshape.430, bf16[]{:T(256)} %constant.55.clone.1), kind=kCustom, calls=%fused_computation.98 | custom fusion | bytes 2267648 | tf_op jit(solution)/shard_map/scatter | solution.py:89
  117.2 4.6 all-to-all-start
  127.8 5.5 mul.277
  137.2 15.1 %gather_fusion.2 = f32[1182]{0:T(1024)S(1)} fusion(f32[591,4]{0,1:T(4,128)S(1)} %fusion.75, s32[1182]{0:T(1024)S(1)} %reshape.420), kind=kCustom, calls=%fused_computation.2 | custom fusion | bytes 18912 | tf_op jit(solution)/shard_map/jit(take_along_axis)/gather | solution.py:114
  152.3 14.2 %scatter_custom_fusion.1 = bf16[1476,768]{1,0:T(8,128)(2,1)S(1)} fusion(s32[1182]{0:T(1024)S(1)} %get-tuple-element.23, f32[1182,768]{1,0:T(8,128)} %mul.277, f32[1182]{0:T(1024)S(1)} %select_select_fusion.1, bf16[]{:T(256)} %constant.55.clone.1), kind=kCustom, calls=%fused_computation.60 | custom fusion | flops 1815552 | bytes 5906434 | tf_op jit(solution)/shard_map/scatter | solution.py:132
  168.5 6.3 all-to-all-done
  178.9 4.0 fusion.48
  185.1 12.8 %convolution_bitcast_fusion = f32[4,1,369,768]{3,2,0,1:T(8,128)} fusion(bf16[1,768,768]{2,1,0:T(8,128)(2,1)S(1)} %copy-done, f32[4,369,768]{2,1,0:T(8,128)S(1)} %fusion.48), kind=kOutput, calls=%fused_computation.49 | convolution fusion | flops 1814842368 | bytes 10248192 | tf_op jit(solution)/shard_map/sjcf,jfd->sjcd/dot_general | solution.py:96
  197.9 6.6 copy.113
  204.5 26.2 %all-to-all-done.2 = bf16[4,369,768]{2,1,0:T(8,128)(2,1)S(1)} async-done(((bf16[4,369,768]{2,1,0:T(8,128)(2,1)}), bf16[4,369,768]{2,1,0:T(8,128)(2,1)S(1)}, u32[]{:S(2)}, u32[]{:S(2)}) %all-to-all-start.2) | async-done | bytes 2267168 | tf_op jit(solution)/shard_map/all_to_all | solution.py:135
  230.7 13.6 %fusion.6 = bf16[4,1,369,768]{3,2,0,1:T(8,128)(2,1)S(1)} fusion(f32[4,369,768]{2,1,0:T(8,128)} %copy-done.58, bf16[4,369,768]{2,1,0:T(8,128)(2,1)S(1)} %all-to-all-done.2, bf16[1,768,768]{2,1,0:T(8,128)(2,1)S(1)} %copy-done), kind=kOutput, calls=%fused_computation.14 | convolution fusion | flops 1822777344 | bytes 10248192 | tf_op jit(solution)/shard_map/sjcd,jfd->sjcf/dot_general | solution.py:137
  245.7 4.2 fusion.26
  249.8 6.7 copy.119
  256.5 314.8 %all-reduce.19 = (bf16[4,1,369,768]{2,0,1,3:T(4,128)(2,1)}, bf16[4,1,369,768]{2,0,1,3:T(4,128)(2,1)}) all-reduce(f32[4,1,369,768]{2,0,1,3:T(4,128)} %copy.113, f32[4,1,369,768]{2,0,1,3:T(4,128)} %copy.119), channel_id=2, replica_groups=mesh['dp'=2,'expert'=4,'tensor'=4] {'tensor'}, use_global_device_ids=true, to_apply=%region_10.11.clone | all-reduce | flops 2267136 | bytes 13602816
  572.7 15.9 %all_to_all.20 = bf16[4,369,192]{1,2,0:T(8,128)(2,1)S(1)} all-to-all(bf16[4,369,192]{1,2,0:T(8,128)(2,1)S(1)} %copy.114), channel_id=1, replica_groups=mesh['dp'=2,'expert'=4,'tensor'=4] {'expert'}, dimensions={0} | all-to-all | bytes 1133568 | tf_op jit(solution)/shard_map/all_to_all | solution.py:102
  600.2 9.8 %all-to-all-done.3 = bf16[4,369,192]{1,2,0:T(8,128)(2,1)S(1)} async-done(((bf16[4,369,192]{1,2,0:T(8,128)(2,1)}), bf16[4,369,192]{1,2,0:T(8,128)(2,1)S(1)}, u32[]{:S(2)}, u32[]{:S(2)}) %all-to-all-start.3) | async-done | bytes 566816 | tf_op jit(solution)/shard_map/all_to_all | solution.py:153
  611.3 5.4 fusion.38
  616.7 13.3 %fusion.41 = bf16[1,768,768]{2,1,0:T(8,128)(2,1)} fusion(bf16[4,369,768]{2,1,0:T(8,128)(2,1)S(1)} %all-to-all-done.2, f32[4,369,768]{2,1,0:T(8,128)} %copy-done.58), kind=kOutput, calls=%fused_computation.77 | convolution fusion | flops 1815432192 | bytes 7981056 | tf_op jit(solution)/shard_map/sjcf,sjcd->jfd/dot_general | solution.py:140
  630.4 5.3 reshape.451
  638.5 27.1 %all-gather.5.cloned.1.call-done = bf16[4,369,768]{1,0,2:T(4,128)(2,1)} async-done(((bf16[4,369,192]{1,0,2:T(4,128)(2,1)}), bf16[4,369,768]{1,0,2:T(4,128)(2,1)}) %all-gather.5.cloned.1.call-update) | async-done | bytes 2267152 | tf_op jit(solution)/shard_map/all_gather | solution.py:160
  665.6 5.3 reshape.452
  670.9 4.2 copy.142
  675.2 4.9 gather_fusion
  680.1 7.7 gather_fusion.1
  687.7 5.3 reshape.403
  693.0 5.1 reshape.401
  698.1 11.0 %multiply_reduce_fusion = (f32[591,2]{1,0:T(8,128)S(1)}, f32[591,768]{1,0:T(8,128)}) fusion(f32[591,2,768]{2,1,0:T(2,128)} %reshape.401, f32[591,768]{1,0:T(8,128)S(1)} %copy-done.10, f32[591,2]{1,0:T(8,128)S(1)} %select_select_fusion), kind=kLoop, calls=%fused_computation.33 | loop fusion | flops 3176034 | bytes 7271664 | tf_op jit(solution)/shard_map/reduce_sum | solution.py:118
  709.7 6.6 multiply_reduce_fusion.1
  742.7 35.6 %all-reduce.14.cloned.1.call-done = bf16[591,768]{1,0:T(8,128)(2,1)} async-done(((bf16[591,768]{1,0:T(8,128)(2,1)}), bf16[591,768]{1,0:T(8,128)(2,1)}) %all-reduce.14.cloned.1.call-update) | async-done | bytes 907792 | tf_op jit(solution)/shard_map/psum | solution.py:216
  787.0 30.9 %all-reduce.2 = (f32[768,4]{0,1:T(4,128)}, f32[768]{0:T(1024)}, f32[768]{0:T(1024)}, f32[4]{0:T(128)S(1)}, f32[4]{0:T(128)S(1)}) all-reduce(f32[768,4]{0,1:T(4,128)S(1)} %fusion.92, f32[768]{0:T(1024)S(1)} %get-tuple-element.14, f32[768]{0:T(1024)S(1)} %get-tuple-element.10, ...), channel_id=1, replica_groups=mesh['dp'=2,'expert'=4,'tensor'=4] {'dp','expert'}, use_global_device_ids=true, to_apply=%region_26.27 | all-reduce | flops 4616 | bytes 36928 | tf_op jit(solution)/shard_map/psum | solution.py:224
  819.1 30.1 %all-reduce.16.cloned.1.call-done = (f32[3,768,192]{1,2,0:T(8,128)}, f32[192,768]{1,0:T(8,128)}) async-done(((f32[3,768,192]{1,2,0:T(8,128)}, f32[192,768]{1,0:T(8,128)}), (f32[3,768,192]{1,2,0:T(8,128)}, f32[192,768]{1,0:T(8,128)})) %all-reduce.16.cloned.1.call-update) | async-done | bytes 2359312 | tf_op jit(solution)/shard_map/psum | solution.py:224
  (241 shorter events, 110.1 us)
Async XLA Ops:
  7.2 177.9 %copy-start = (bf16[1,768,768]{2,1,0:T(8,128)(2,1)S(1)}, bf16[1,768,768]{2,1,0:T(8,128)(2,1)}, u32[]{:S(2)}) copy-start(bf16[1,768,768]{2,1,0:T(8,128)(2,1)} %param.19) | copy-start | bytes 3538948
  7.2 88.7 %all-reduce.12.cloned.1.call-start = ((), (), s32[]{:S(2)}) async-start(), calls=%async_computation.4 | async-start | bytes 3637248 | tf_op jit(solution)/shard_map/psum | solution.py:76
  11.8 84.1 %copy-start.4 = (f32[591,768]{1,0:T(8,128)}, f32[591,768]{1,0:T(8,128)S(1)}, u32[]{:S(2)}) copy-start(f32[591,768]{1,0:T(8,128)S(1)} %reshape.400) | copy-start | bytes 5446660
  18.7 9.3 %copy-start.16 = (bf16[3,197,3,64]{1,0,3,2:T(4,128)(2,1)}, bf16[3,197,3,64]{1,0,3,2:T(4,128)(2,1)S(1)}, u32[]{:S(2)}) copy-start(bf16[3,197,3,64]{1,0,3,2:T(4,128)(2,1)S(1)} %squeeze.9) | copy-start | bytes 680836
  28.0 71.6 %copy-start.44 = (f32[768]{0:T(1024)S(1)}, f32[768]{0:T(1024)}, u32[]{:S(2)}) copy-start(f32[768]{0:T(1024)} %param.21) | copy-start | bytes 9220
  117.2 57.6 %all-to-all-start = ((bf16[4,369,768]{2,1,0:T(8,128)(2,1)}), bf16[4,369,768]{2,1,0:T(8,128)(2,1)}, u32[]{:S(2)}, u32[]{:S(2)}) async-start(bf16[4,369,768]{2,1,0:T(8,128)(2,1)} %reshape.386), calls=%async_computation | async-start | bytes 4620288 | tf_op jit(solution)/shard_map/all_to_all | solution.py:92
  124.7 8.6 copy-start.9
  174.8 55.9 %all-to-all-start.2 = ((bf16[4,369,768]{2,1,0:T(8,128)(2,1)}), bf16[4,369,768]{2,1,0:T(8,128)(2,1)S(1)}, u32[]{:S(2)}, u32[]{:S(2)}) async-start(bf16[4,369,768]{2,1,0:T(8,128)(2,1)} %reshape.394), calls=%async_computation.2 | async-start | bytes 4620288 | tf_op jit(solution)/shard_map/all_to_all | solution.py:135
  178.4 451.9 %all-gather.3.cloned.1.call-start = ((), (), s32[]{:S(2)}) async-start(), calls=%async_computation.5 | async-start | bytes 2949120 | tf_op jit(solution)/shard_map/all_gather | solution.py:109
  230.7 15.0 %copy-start.54 = (bf16[1,768,768]{2,1,0:T(8,128)(2,1)S(1)}, bf16[1,768,768]{2,1,0:T(8,128)(2,1)}, u32[]{:S(2)}) copy-start(bf16[1,768,768]{2,1,0:T(8,128)(2,1)} %param.18) | copy-start | bytes 3538948
  571.3 24.5 %copy-start.50 = (pred[3,197,2]{1,2,0:T(4,128)(4,1)S(1)}, pred[3,197,2]{1,2,0:T(4,128)(4,1)}, u32[]{:S(2)}) copy-start(pred[3,197,2]{1,2,0:T(4,128)(4,1)} %copy-done.49) | copy-start | bytes 3550
  571.3 24.5 %copy-start.34 = (s32[3,197,2]{1,0,2:T(4,128)S(1)}, s32[3,197,2]{1,0,2:T(4,128)}, u32[]{:S(2)}) copy-start(s32[3,197,2]{1,0,2:T(4,128)} %copy-done.33) | copy-start | bytes 14188
  571.3 26.7 %copy-start.48 = (s32[1182]{0:T(1024)S(1)}, s32[1182]{0:T(1024)}, u32[]{:S(2)}) copy-start(s32[1182]{0:T(1024)} %get-tuple-element.22) | copy-start | bytes 14188
  592.1 17.9 %all-to-all-start.3 = ((bf16[4,369,192]{1,2,0:T(8,128)(2,1)}), bf16[4,369,192]{1,2,0:T(8,128)(2,1)S(1)}, u32[]{:S(2)}, u32[]{:S(2)}) async-start(bf16[4,369,192]{1,2,0:T(8,128)(2,1)} %copy.120), calls=%async_computation.3 | async-start | bytes 1179648 | tf_op jit(solution)/shard_map/all_to_all | solution.py:153
  595.6 70.1 %all-gather.5.cloned.1.call-start = ((), (), s32[]{:S(2)}) async-start(), calls=%async_computation.6 | async-start | bytes 2949120 | tf_op jit(solution)/shard_map/all_gather | solution.py:160
  611.2 116.9 %all-reduce.18.cloned.1.call-start = ((), (), s32[]{:S(2)}) async-start(), calls=%async_computation.9 | async-start | bytes 4718592 | tf_op jit(solution)/shard_map/psum | solution.py:238
  630.1 148.2 %all-reduce.14.cloned.1.call-start = ((), (), s32[]{:S(2)}) async-start(), calls=%async_computation.7 | async-start | bytes 1818624 | tf_op jit(solution)/shard_map/psum | solution.py:216
  687.7 10.4 %copy-start.10 = (f32[591,768]{1,0:T(8,128)S(1)}, f32[591,768]{1,0:T(8,128)}, u32[]{:S(2)}) copy-start(f32[591,768]{1,0:T(8,128)} %copy-done.9) | copy-start | bytes 5446660
  698.1 11.4 %copy-start.28 = (f32[591,4]{0,1:T(4,128)S(1)}, f32[591,4]{0,1:T(4,128)}, u32[]{:S(2)}) copy-start(f32[591,4]{0,1:T(4,128)} %copy-done.27) | copy-start | bytes 28372
  698.1 11.4 %copy-start.30 = (f32[591]{0:T(1024)S(1)}, f32[591]{0:T(1024)}, u32[]{:S(2)}) copy-start(f32[591]{0:T(1024)} %copy-done.29) | copy-start | bytes 7096
  698.1 11.4 %copy-start.36 = (f32[591]{0:T(1024)S(1)}, f32[591]{0:T(1024)}, u32[]{:S(2)}) copy-start(f32[591]{0:T(1024)} %copy-done.35) | copy-start | bytes 7096
  698.1 11.5 %copy-start.22 = (f32[591,2]{1,0:T(8,128)S(1)}, f32[591,2]{1,0:T(8,128)}, u32[]{:S(2)}) copy-start(f32[591,2]{1,0:T(8,128)} %copy.123) | copy-start | bytes 14188
  709.7 7.8 copy-start.8
  709.7 7.8 copy-start.11
  727.7 8.6 copy-start.14
  727.7 121.4 %all-reduce.16.cloned.1.call-start = ((), (), s32[]{:S(2)}) async-start(), calls=%async_computation.8 | async-start | bytes 4718592 | tf_op jit(solution)/shard_map/psum | solution.py:224
  728.1 8.4 copy-start.20
  731.0 8.3 copy-start.5
  731.0 8.3 copy-start.38
  731.0 8.3 copy-start.40
  731.0 8.3 copy-start.47
  780.4 73.5 %copy-start.1 = (bf16[1,768,768]{2,1,0:T(8,128)(2,1)S(1)}, bf16[1,768,768]{2,1,0:T(8,128)(2,1)}, u32[]{:S(2)}) copy-start(bf16[1,768,768]{2,1,0:T(8,128)(2,1)} %param.19) | copy-start | bytes 3538948
  (36 other events, 120.8 us)
Sparse Core Ops, SparseCore 0:
  28.2 67.7 all-reduce.11
  590.0 35.5 all-gather.2
  628.1 37.4 all-gather.4
  668.6 21.6 all-reduce.17
  727.9 50.4 all-reduce.13
  781.3 67.7 all-reduce.15
where the time goes:
time: 872 us; the launch traced here: 862 us
  blocking collectives  362 us (42%)
  waiting for transfers between devices  202 us (23%)
  local copies, waits for them, and re-layouts  139 us (16%)
  matrix products  74 us (8%)
  other arithmetic  54.2 us (6%)
  between operations  18 us (2%)
  starting transfers between devices  13 us (1%)
    unnamed x1, blocking collectives  315 us
    psum x1, waiting for transfers between devices, body(): residual = inputs + lax.psum(attn_part, 'tensor')  66.8 us
    psum x1, waiting for transfers between devices, body(): lax.psum(entered_part.astype(jnp.bfloat16), 'tensor').astype(jnp.float32)  35.6 us
    psum x1, blocking collectives, body(): lax.psum((grad_qkv, grad_out, grad_router, grad_gain_attention, grad_gain...  30.9 us
    psum x1, waiting for transfers between devices, body(): lax.psum((grad_qkv, grad_out, grad_router, grad_gain_attention, grad_gain...  30.1 us
    all_gather x1, waiting for transfers between devices, body(): lax.all_gather(buffer_back, 'tensor', axis=2, tiled=True)  27.1 us
    all_to_all x1, waiting for transfers between devices, body(): lax.all_to_all(grad_send, 'expert', split_axis=0, concat_axis=0, tiled=True)  26.2 us
  transfers between devices with their start and end apart: 9, of which 7 were waited for; matrix products, arithmetic and copies ran while one was open for 22% of the time, Pallas kernels for 0%

commit v1 on v0

--- a/solution.py
+++ b/solution.py
@@ -1,6 +1,11 @@
+import functools
+import math
+
 import jax
 import jax.numpy as jnp
 from jax import lax
+from jax.experimental import pallas as pl
+from jax.experimental.pallas import tpu as pltpu
 from jax.sharding import PartitionSpec as P
 
 HD = 64
@@ -254,6 +259,772 @@
     )
 
 
+NN = ((1,), (0,))
+NT = ((1,), (1,))
+TN = ((0,), (0,))
+LANES = 128
+SMALL = 8
+VMEM_BYTES = 56 << 20
+
+
+def round_up(value, step):
+    return -(-value // step) * step
+
+
+def contract(a, b, dims):
+    return lax.dot_general(a, b, (dims, ((), ())), preferred_element_type=jnp.float32)
+
+
+def fixed(shape):
+    return pl.BlockSpec(shape, lambda *_: (0,) * len(shape))
+
+
+def kernel_call(kernel, name, position, args, outs, scratch=(), blocks=None, grid=(1,), flops=0):
+    bytes_moved = sum(a.size * a.dtype.itemsize for a in args)
+    bytes_moved += sum(o.size * o.dtype.itemsize for o in outs)
+    return pl.pallas_call(
+        kernel,
+        grid_spec=pltpu.PrefetchScalarGridSpec(
+            num_scalar_prefetch=1,
+            grid=grid,
+            in_specs=[fixed((blocks or {}).get(i, a.shape)) for i, a in enumerate(args)],
+            out_specs=[fixed(o.shape) for o in outs],
+            scratch_shapes=list(scratch),
+        ),
+        out_shape=list(outs),
+        compiler_params=pltpu.CompilerParams(vmem_limit_bytes=VMEM_BYTES),
+        cost_estimate=pl.CostEstimate(flops=flops, bytes_accessed=bytes_moved, transcendentals=0),
+        name=name,
+    )(position, *args)
+
+
+def like(shape, dtype):
+    return jax.ShapeDtypeStruct(shape, dtype)
+
+
+def live_rows(shape, limit, offset=0):
+    return lax.broadcasted_iota(jnp.int32, shape, 0) + offset < limit
+
+
+def head_masks(rows, heads):
+    lane = lax.broadcasted_iota(jnp.int32, (rows, heads * HD), 1)
+    return [(lane >= h * HD) & (lane < (h + 1) * HD) for h in range(heads)]
+
+
+def keep_lanes(value, mask):
+    return jnp.where(mask, value, jnp.zeros_like(value))
+
+
+def split_high_low(value):
+    high = value.astype(jnp.bfloat16)
+    return high, (value - high.astype(jnp.float32)).astype(jnp.bfloat16)
+
+
+def image_rows(ref, i, seq_len):
+    values = ref[i].astype(jnp.float32)
+    return jnp.where(live_rows(values.shape, seq_len), values, 0.0)
+
+
+def chunk_kernel(seq_len, pos_ref, tok_ref, cot_ref, kept_ref, x_ref, pay_ref, flat_ref):
+    images, rows, width = tok_ref.shape
+    chunk = x_ref.shape[0]
+    start = pl.multiple_of(pos_ref[2] * chunk, 16)
+    for source, target in ((tok_ref, x_ref), (cot_ref, pay_ref)):
+        flat_ref[images * seq_len :, :] = jnp.zeros(
+            (flat_ref.shape[0] - images * seq_len, width), jnp.float32
+        )
+        for i in range(images):
+            flat_ref[pl.ds(i * seq_len, rows), :] = image_rows(source, i, seq_len)
+        target[:, :width] = flat_ref[pl.ds(start, chunk), :].astype(jnp.bfloat16)
+    pay_ref[:, width:] = kept_ref[pl.ds(start, chunk), :]
+
+
+def attention_kernel(
+    seq_len, heads, pos_ref, tok_ref, gain_ref, w_ref, wo_ref, qkv_ref, lse_ref, att_ref, part_ref, flat_ref
+):
+    images, rows, width = qkv_ref.shape[1], qkv_ref.shape[2], heads * HD
+    masks = head_masks(rows, heads)
+    keys_live = lax.broadcasted_iota(jnp.int32, (rows, rows), 1) < seq_len
+    lane = lax.broadcasted_iota(jnp.int32, (rows, LANES), 1)
+    flat_ref[images * seq_len :, :] = jnp.zeros(
+        (flat_ref.shape[0] - images * seq_len, width), jnp.float32
+    )
+    for i in range(images):
+        entered = normalize(image_rows(tok_ref, i, seq_len), gain_ref[...])[2].astype(jnp.bfloat16)
+        q, k, v = (
+            contract(entered, w_ref[c * width : (c + 1) * width, :], NT).astype(jnp.bfloat16)
+            for c in range(3)
+        )
+        qkv_ref[0, i], qkv_ref[1, i], qkv_ref[2, i] = q, k, v
+        attended = jnp.zeros((rows, width), jnp.float32)
+        lse_all = jnp.zeros((rows, LANES), jnp.float32)
+        for h in range(heads):
+            scores = contract(keep_lanes(q, masks[h]), k, NT) * (HD ** (-0.5))
+            scores = jnp.where(keys_live, scores, -1e30)
+            top = jnp.max(scores, axis=-1, keepdims=True)
+            lse = top + jnp.log(jnp.sum(jnp.exp(scores - top), axis=-1, keepdims=True))
+            probs = jnp.exp(scores - lse).astype(jnp.bfloat16)
+            attended = attended + contract(probs, keep_lanes(v, masks[h]), NN)
+            lse_all = jnp.where(lane == h, lse, lse_all)
+        lse_ref[i] = lse_all
+        flat_ref[pl.ds(i * seq_len, rows), :] = jnp.where(
+            live_rows(attended.shape, seq_len), attended, 0.0
+        )
+    att = flat_ref[...].astype(jnp.bfloat16)
+    att_ref[...] = att
+    part_ref[...] = contract(att, wo_ref[...], NN).astype(jnp.bfloat16)
+
+
+def route_kernel(experts, pos_ref, got_ref, x_ref, gain_ref, router_ref, res_ref, routed_ref, prob_ref):
+    residual = x_ref[...].astype(jnp.float32)
+    for j in range(got_ref.shape[0]):
+        residual = residual + got_ref[j].astype(jnp.float32)
+    res_ref[...] = residual
+    routed = normalize(residual, gain_ref[...])[2].astype(jnp.bfloat16)
+    routed_ref[...] = routed
+    prob_ref[...] = route_probs(routed, router_ref[...], experts)
+
+
+def route_probs(rows, router, experts):
+    logits = contract(rows, router, NT)
+    lane = lax.broadcasted_iota(jnp.int32, logits.shape, 1)
+    logits = jnp.where(lane < experts, logits, -1e30)
+    weight = jnp.exp(logits - jnp.max(logits, axis=-1, keepdims=True))
+    return weight / jnp.sum(weight, axis=-1, keepdims=True)
+
+
+def gelu_parts(x):
+    square = jnp.exp(-0.5 * x * x)
+    t = 1.0 / (1.0 + (0.3275911 * 0.5**0.5) * jnp.abs(x))
+    poly = 0.5 * 1.061405429
+    for coefficient in (-1.453152027, 1.421413741, -0.284496736, 0.254829592):
+        poly = poly * t + 0.5 * coefficient
+    tail = poly * t * square
+    share = jnp.where(x < 0, tail, 1.0 - tail)
+    return x * share, share + x * square * (0.5 / math.pi) ** 0.5
+
+
+def expert_kernel(experts, owners, *refs):
+    pos_ref, *blocks = refs[: 1 + owners]
+    pay_ref, router_ref, w0_ref, w1a_ref, w1b_ref, w2_ref, w3_ref = refs[1 + owners : 8 + owners]
+    hidden_ref, pre_ref, x_ref, rg_ref, gated_ref, back_ref = refs[8 + owners : 14 + owners]
+    w_ref, gate_ref, acc_ref, back_acc = refs[14 + owners :]
+    chunk, width = blocks[0].shape
+    part_rows = w_ref.shape[1] // 2
+    step = pl.program_id(0)
+
+    def load_halves(first, second):
+        w_ref[:, :part_rows, :] = first
+        w_ref[:, part_rows:, :] = second
+
+    @pl.when(step == 0)
+    def _():
+        w_ref[...] = w0_ref[...]
+        me = pos_ref[1]
+        for k in range(owners):
+            here = pl.ds(k * chunk, chunk)
+            rows = blocks[k][...]
+            x_ref[here, :] = rows
+            source = pl.ds(pl.multiple_of(lax.rem(me - k + owners, owners) * chunk, 16), chunk)
+            prob = route_probs(rows, router_ref[...], experts)
+            lane = lax.broadcasted_iota(jnp.int32, prob.shape, 1)
+            kept = pay_ref[source, width:].astype(jnp.float32)
+            kept = jnp.sum(jnp.where(lane == me, kept, 0.0), axis=-1, keepdims=True)
+            gate = jnp.sum(jnp.where(lane == me, prob, 0.0), axis=-1, keepdims=True) * kept
+            gate_ref[here, :LANES] = jnp.broadcast_to(gate, (chunk, LANES))
+            gate_ref[here, LANES:] = jnp.broadcast_to(kept, (chunk, LANES))
+            rg_ref[here, :] = (gate * pay_ref[source, :width].astype(jnp.float32)).astype(
+                jnp.bfloat16
+            )
+        acc_ref[...] = jnp.zeros_like(acc_ref)
+        back_acc[...] = jnp.zeros_like(back_acc)
+
+    @pl.when(step == 1)
+    def _():
+        load_halves(w1a_ref[...], w1b_ref[...])
+
+    @pl.when(step == 2)
+    def _():
+        load_halves(w2_ref[0], w2_ref[1])
+
+    @pl.when(step == 3)
+    def _():
+        load_halves(w3_ref[0], w3_ref[1])
+
+    before = contract(x_ref[...], w_ref[0], NT)
+    value, slope = gelu_parts(before)
+    hidden = value.astype(jnp.bfloat16)
+    hidden_ref[...] = hidden
+    acc_ref[...] += contract(hidden, w_ref[1], NN)
+    pre = (contract(rg_ref[...], w_ref[1], NT) * slope).astype(jnp.bfloat16)
+    pre_ref[...] = pre
+    back_acc[...] += contract(pre, w_ref[0], NN)
+
+    @pl.when(step == pl.num_programs(0) - 1)
+    def _():
+        me = pos_ref[1]
+        for k in range(owners):
+            here = pl.ds(k * chunk, chunk)
+            source = pl.ds(pl.multiple_of(lax.rem(me - k + owners, owners) * chunk, 16), chunk)
+            part = acc_ref[here, :]
+            gated_ref[here, :] = (gate_ref[here, 0:1] * part).astype(jnp.bfloat16)
+            back_ref[here, :width] = back_acc[here, :]
+            inner = jnp.sum(
+                part * pay_ref[source, :width].astype(jnp.float32), axis=-1, keepdims=True
+            )
+            back_ref[here, width:] = gate_ref[here, LANES:] * inner
+
+
+def expert_pass(position, blocks, payload, router, weights, experts):
+    chunk, width = blocks[0].shape
+    owners = len(blocks)
+    count, tile = owners * chunk, weights[0].shape[1]
+    args = [*blocks, payload, router, *weights]
+    outs = [
+        like((count, 4 * tile), jnp.bfloat16),
+        like((count, 4 * tile), jnp.bfloat16),
+        like((count, width), jnp.bfloat16),
+        like((count, width), jnp.bfloat16),
+        like((count, width), jnp.bfloat16),
+        like((count, width + LANES), jnp.float32),
+    ]
+    column = pl.BlockSpec((count, tile), lambda j, *_: (0, j))
+    return pl.pallas_call(
+        functools.partial(expert_kernel, experts, owners),
+        grid_spec=pltpu.PrefetchScalarGridSpec(
+            num_scalar_prefetch=1,
+            grid=(4,),
+            in_specs=[fixed(a.shape) for a in args],
+            out_specs=[column, column] + [fixed(o.shape) for o in outs[2:]],
+            scratch_shapes=[
+                pltpu.VMEM((2, tile, width), jnp.bfloat16),
+                pltpu.VMEM((count, 2 * LANES), jnp.float32),
+                pltpu.VMEM((count, width), jnp.float32),
+                pltpu.VMEM((count, width), jnp.float32),
+            ],
+        ),
+        out_shape=outs,
+        compiler_params=pltpu.CompilerParams(vmem_limit_bytes=VMEM_BYTES),
+        cost_estimate=pl.CostEstimate(
+            flops=8 * count * width * 4 * tile,
+            bytes_accessed=16 * width * tile + 12 * count * width + 16 * count * tile,
+            transcendentals=2 * count * 4 * tile,
+        ),
+        name="experts",
+    )(position, *args)
+
+
+def join_kernel(pos_ref, back_ref, other_ref, gated_ref, gated_other_ref, *outs):
+    owners = len(outs) // 2
+    chunk, width = outs[owners].shape
+    for k in range(owners):
+        here = pl.ds(k * chunk, chunk)
+        total = back_ref[here, :] + other_ref[here, :]
+        outs[k][:, :width] = total[:, :width].astype(jnp.bfloat16)
+        outs[k][:, width : width + LANES], outs[k][:, width + LANES :] = split_high_low(
+            total[:, width:]
+        )
+        outs[owners + k][...] = (
+            gated_ref[here, :].astype(jnp.float32) + gated_other_ref[here, :].astype(jnp.float32)
+        ).astype(jnp.bfloat16)
+
+
+def expert_grad_kernel(pos_ref, xa, xb, pa, pb, ha, hb, ra, rb, *outs):
+    step = pl.program_id(0)
+    part_rows = outs[0].shape[2]
+    grad_in = contract(pa[...], xa[...], TN) + contract(pb[...], xb[...], TN)
+    grad_in = grad_in.astype(jnp.bfloat16)
+    grad_out = contract(ha[...], ra[...], TN) + contract(hb[...], rb[...], TN)
+    grad_out = grad_out.astype(jnp.bfloat16)
+    for j, out in enumerate(outs):
+
+        @pl.when(step == j)
+        def _(out=out):
+            for s in range(2):
+                here = slice(s * part_rows, (s + 1) * part_rows)
+                out[s, 0] = grad_in[here]
+                out[s, 1] = grad_out[here]
+
+
+def expert_grads(position, rows, pre, hidden, row_grad):
+    count, width = rows[0].shape
+    tile = pre[0].shape[1] // 4
+    column = pl.BlockSpec((count, tile), lambda j, *_: (0, j))
+    outs = [like((2, 2, tile // 2, width), jnp.bfloat16)] * 4
+    return pl.pallas_call(
+        expert_grad_kernel,
+        grid_spec=pltpu.PrefetchScalarGridSpec(
+            num_scalar_prefetch=1,
+            grid=(4,),
+            in_specs=[fixed((count, width))] * 2 + [column] * 4 + [fixed((count, width))] * 2,
+            out_specs=[fixed(o.shape) for o in outs],
+        ),
+        out_shape=outs,
+        compiler_params=pltpu.CompilerParams(vmem_limit_bytes=VMEM_BYTES),
+        cost_estimate=pl.CostEstimate(
+            flops=8 * count * width * 4 * tile,
+            bytes_accessed=16 * width * tile + 8 * count * width + 32 * count * tile,
+            transcendentals=0,
+        ),
+        name="expert_grads",
+    )(position, *rows, *pre, *hidden, *row_grad)
+
+
+def route_back_kernel(
+    experts, token_rows, owners, pos_ref, *refs
+):
+    backs = refs[:owners]
+    prob_ref, res_ref, pay_ref, router_ref, gain_ref, count_ref = refs[owners : owners + 6]
+    grad_ref, up_ref, small_ref = refs[owners + 6 :]
+    chunk, width = res_ref.shape
+    prob = prob_ref[...]
+    lane = lax.broadcasted_iota(jnp.int32, prob.shape, 1)
+    route_grad = jnp.zeros_like(prob)
+    routed_grad = jnp.zeros((chunk, width), jnp.float32)
+    for k, back in enumerate(backs):
+        owner = lax.rem(pos_ref[1] + k, owners)
+        inner = back[:, width : width + LANES].astype(jnp.float32)
+        inner = inner + back[:, width + LANES :].astype(jnp.float32)
+        route_grad = jnp.where(lane == owner, inner, route_grad)
+        routed_grad = routed_grad + back[:, :width].astype(jnp.float32)
+    mean = jnp.sum(route_grad * prob, axis=-1, keepdims=True)
+    logit_grad = (prob * (route_grad - mean)).astype(jnp.bfloat16)
+    routed_grad = routed_grad + contract(logit_grad, router_ref[...], NN)
+    normed, inverse, mixed = normalize(res_ref[...], gain_ref[...])
+    from_norm, gain_grad = normalize_back(routed_grad, normed, inverse, gain_ref[...])
+    total = pay_ref[:, :width].astype(jnp.float32) + from_norm
+    grad_ref[...] = total
+    up_ref[...] = total.astype(jnp.bfloat16)
+    live = live_rows(prob.shape, token_rows, pos_ref[2] * chunk)
+    prob_sum = jnp.sum(jnp.where(live, prob, 0.0), axis=0, keepdims=True)
+    grad_router = contract(logit_grad, mixed.astype(jnp.bfloat16), TN)
+    small_ref[0:SMALL, :] = grad_router[0:SMALL]
+    small_ref[experts : experts + 1, :] = gain_grad[None]
+    small_ref[experts + 1 : experts + 2, :] = jnp.zeros((1, width), jnp.float32)
+    small_ref[experts + 1 : experts + 2, :LANES] = prob_sum
+    small_ref[experts + 2 : experts + 3, :] = count_ref[...]
+
+
+def attention_back_kernel(
+    seq_len, heads, owners, pos_ref, tok_ref, gain_ref, w_ref, wo_ref, qkv_ref, lse_ref, att_ref,
+    up_ref, small_ref, keep_ref, send_ref, part_ref, hg_ref, flat_ref, big_ref,
+):
+    images, rows, width = qkv_ref.shape[1], qkv_ref.shape[2], heads * HD
+    scale = HD ** (-0.5)
+    padded, model = up_ref.shape
+    tensors = part_ref.shape[0]
+    chunk = padded // tensors
+    masks = head_masks(rows, heads)
+    keys_live = lax.broadcasted_iota(jnp.int32, (rows, rows), 1) < seq_len
+    lane = lax.broadcasted_iota(jnp.int32, (rows, LANES), 1)
+    up = up_ref[...]
+    hg_ref[0:padded, :] = contract(up, wo_ref[...], NT)
+    hg_ref[padded:, :] = jnp.zeros((hg_ref.shape[0] - padded, width), jnp.float32)
+    big_ref[3 * width :, :] = contract(att_ref[...], up, TN)
+    flat_ref[images * seq_len :, :] = jnp.zeros(
+        (flat_ref.shape[0] - images * seq_len, model), jnp.float32
+    )
+    gain_grad = jnp.zeros((1, model), jnp.float32)
+    for i in range(images):
+        normed, _, mixed = normalize(image_rows(tok_ref, i, seq_len), gain_ref[...])
+        entered = mixed.astype(jnp.bfloat16)
+        q, k, v = qkv_ref[0, i], qkv_ref[1, i], qkv_ref[2, i]
+        heads_grad = hg_ref[pl.ds(i * seq_len, rows), :]
+        heads_grad = jnp.where(live_rows(heads_grad.shape, seq_len), heads_grad, 0.0)
+        heads_grad = heads_grad.astype(jnp.bfloat16)
+        dq = jnp.zeros((rows, width), jnp.float32)
+        dk, dv = dq, dq
+        for h in range(heads):
+            q_h, k_h = keep_lanes(q, masks[h]), keep_lanes(k, masks[h])
+            up_h = keep_lanes(heads_grad, masks[h])
+            scores = contract(q_h, k, NT) * scale
+            lse = jnp.sum(jnp.where(lane == h, lse_ref[i], 0.0), axis=-1, keepdims=True)
+            probs = jnp.where(keys_live, jnp.exp(scores - lse), 0.0)
+            prob_grad = contract(up_h, v, NT)
+            total = jnp.sum(prob_grad * probs, axis=-1, keepdims=True)
+            score_grad = (probs * (prob_grad - total)).astype(jnp.bfloat16)
+            dv = dv + contract(probs.astype(jnp.bfloat16), up_h, TN)
+            dq = dq + contract(score_grad, k_h, NN)
+            dk = dk + contract(score_grad, q_h, TN)
+        grads = [g.astype(jnp.bfloat16) for g in (dq * scale, dk * scale, dv)]
+        part = jnp.zeros((rows, model), jnp.float32)
+        for c in range(3):
+            here = slice(c * width, (c + 1) * width)
+            part = part + contract(grads[c], w_ref[here, :], NN)
+            if i == 0:
+                big_ref[here, :] = contract(grads[c], entered, TN)
+            else:
+                big_ref[here, :] += contract(grads[c], entered, TN)
+        gain_grad = gain_grad + jnp.sum(part * normed, axis=0, keepdims=True)
+        flat_ref[pl.ds(i * seq_len, rows), :] = part
+    high, low = split_high_low(
+        jnp.concatenate([small_ref[0 : SMALL - 1, :], gain_grad], axis=0)
+    )
+    for j in range(tensors):
+        part_ref[j, 0:chunk, :] = flat_ref[j * chunk : (j + 1) * chunk, :].astype(jnp.bfloat16)
+        part_ref[j, chunk : chunk + 2 * SMALL, :] = jnp.concatenate([high, low], axis=0)
+    me, core = pos_ref[1], pos_ref[0]
+    piece = keep_ref.shape[1]
+    for k in range(owners):
+        place = lax.rem(me + k, owners) * piece
+        mine = pl.ds(pl.multiple_of(core * owners * piece + place, 8), piece)
+        other = pl.ds(pl.multiple_of((1 - core) * owners * piece + place, 8), piece)
+        keep_ref[k] = big_ref[mine, :]
+        send_ref[k] = big_ref[other, :].astype(jnp.bfloat16)
+
+
+def norm_back_kernel(pos_ref, got_ref, x_ref, res_ref, gain_ref, grad_ref, small_ref):
+    tensors = got_ref.shape[0]
+    chunk = x_ref.shape[0]
+    upstream = jnp.zeros(x_ref.shape, jnp.float32)
+    small = jnp.zeros(small_ref.shape, jnp.float32)
+    for j in range(tensors):
+        upstream = upstream + got_ref[j, 0:chunk, :].astype(jnp.float32)
+        small = small + got_ref[j, chunk : chunk + SMALL, :].astype(jnp.float32)
+        small = small + got_ref[j, chunk + SMALL :, :].astype(jnp.float32)
+    small_ref[...] = small
+    normed, inverse, _ = normalize(x_ref[...].astype(jnp.float32), gain_ref[...])
+    from_norm = normalize_back(upstream, normed, inverse, gain_ref[...])[0]
+    grad_ref[...] = (res_ref[...] + from_norm).astype(jnp.bfloat16)
+
+
+def add_core_kernel(pos_ref, keep_ref, other_ref, own_ref, *outs):
+    total = keep_ref[...] + other_ref[...].astype(jnp.float32)
+    own_ref[...] = total[0]
+    for k, out in enumerate(outs):
+        out[...] = total[k + 1].astype(jnp.bfloat16)
+
+
+def sum_owner_kernel(pos_ref, own_ref, *refs):
+    *parts, small_ref, out_ref = refs
+    piece = own_ref.shape[0]
+    total = own_ref[...]
+    for part in parts:
+        total = total + part[...].astype(jnp.float32)
+    high, low = split_high_low(small_ref[...])
+    out_ref[0:piece, :] = total.astype(jnp.bfloat16)
+    out_ref[piece:, :] = jnp.concatenate([high, low], axis=0)
+
+
+def spread_kernel(owners, experts, token_total, pos_ref, *refs):
+    blocks = refs[: 2 * owners]
+    qkv_ref, wo_ref, small_ref, loss_ref, big_ref, parts_ref = refs[2 * owners :]
+    piece = blocks[0].shape[0] - 2 * SMALL
+    core, me = pos_ref[0], pos_ref[1]
+    for c in range(2):
+        side = core if c == 0 else 1 - core
+        for k in range(owners):
+            block = blocks[c * owners + k]
+            place = side * owners + lax.rem(me - k + owners, owners)
+            here = pl.ds(pl.multiple_of(place * piece, 8), piece)
+            big_ref[here, :] = block[0:piece, :].astype(jnp.float32)
+            parts_ref[place] = block[piece : piece + SMALL, :].astype(jnp.float32) + block[
+                piece + SMALL :, :
+            ].astype(jnp.float32)
+    rows = qkv_ref.shape[0]
+    qkv_ref[...] = big_ref[0:rows, :]
+    wo_ref[...] = big_ref[rows:, :]
+    small = parts_ref[0]
+    for p in range(1, 2 * owners):
+        small = small + parts_ref[p]
+    small_ref[...] = small
+    product = small[experts + 1 : experts + 2, :LANES] * small[experts + 2 : experts + 3, :LANES]
+    lane = lax.broadcasted_iota(jnp.int32, product.shape, 1)
+    product = jnp.where(lane < experts, product, 0.0)
+    loss = jnp.sum(product, axis=-1, keepdims=True)
+    loss_ref[...] = jnp.broadcast_to(
+        loss * (experts / (2.0 * token_total * token_total)), loss_ref.shape
+    )
+
+
+def images_kernel(seq_len, pos_ref, rows_ref, out_ref, flat_ref):
+    flat_ref[...] = rows_ref[...].astype(jnp.float32)
+    for i in range(out_ref.shape[0]):
+        out_ref[i] = flat_ref[pl.ds(i * seq_len, seq_len), :].astype(out_ref.dtype)
+
+
+def gather_images_kernel(seq_len, pos_ref, *refs):
+    *chunks, out_ref, flat_ref = refs
+    chunk = chunks[0].shape[0]
+    for j, part in enumerate(chunks):
+        here = pl.ds(pl.multiple_of(lax.bitwise_xor(pos_ref[2], j) * chunk, 16), chunk)
+        flat_ref[here, :] = part[...].astype(jnp.float32)
+    for i in range(out_ref.shape[0]):
+        out_ref[i] = flat_ref[pl.ds(i * seq_len, seq_len), :].astype(out_ref.dtype)
+
+
+def weight_out_kernel(pos_ref, mine_ref, other_ref, in_ref, out_ref):
+    first_is_mine = pos_ref[0] == 0
+    half = mine_ref.shape[1]
+    for c in range(2):
+        here = slice(c * half, (c + 1) * half)
+        take = first_is_mine if c == 0 else jnp.logical_not(first_is_mine)
+        grad_in = jnp.where(take, mine_ref[0], other_ref[0]).astype(jnp.float32)
+        in_ref[0, :, here] = grad_in.T
+        out_ref[0, here, :] = jnp.where(take, mine_ref[1], other_ref[1]).astype(jnp.float32)
+
+
+def swap_core(value):
+    return lax.ppermute(value, "dp", [(0, 1), (1, 0)])
+
+
+def ring(value, shift):
+    size = lax.axis_size("expert")
+    return lax.ppermute(value, "expert", [(i, (i + shift) % size) for i in range(size)])
+
+
+def cross(value, bit):
+    size = lax.axis_size("tensor")
+    return lax.ppermute(value, "tensor", [(i, i ^ bit) for i in range(size)])
+
+
+def after(value, *others):
+    return lax.optimization_barrier((value, *others))[0]
+
+
+def dense_body(
+    tokens,
+    cotangent,
+    expert_ids,
+    slot_rank,
+    qkv_weight,
+    out_weight,
+    router_weight,
+    expert_in,
+    expert_out,
+    gain_attention,
+    gain_experts,
+):
+    f32, b16 = jnp.float32, jnp.bfloat16
+    images, seq_len, width = tokens.shape
+    token_rows = images * seq_len
+    local = qkv_weight.shape[2]
+    heads = local // HD
+    experts = router_weight.shape[1]
+    owners = lax.axis_size("expert")
+    tensors = lax.axis_size("tensor")
+    cores = lax.axis_size("dp")
+    chunk = round_up(-(-token_rows // tensors), 16)
+    padded = chunk * tensors
+    rows = round_up(seq_len, 16)
+    flat_rows = padded + 32
+    half = expert_in.shape[2] // cores
+    quarter = half // 2
+    position = jnp.stack(
+        [lax.axis_index("dp"), lax.axis_index("expert"), lax.axis_index("tensor")]
+    ).astype(jnp.int32)
+    my_core = position[0]
+    weight_rows = qkv_weight.transpose(0, 2, 1).reshape(3 * local, width)
+    router_rows = jnp.pad(router_weight.T, ((0, LANES - experts), (0, 0)))
+    gain_one, gain_two = gain_attention[None], gain_experts[None]
+    image_block = (images, rows, width)
+
+    qkv, lse, attended, part = kernel_call(
+        functools.partial(attention_kernel, seq_len, heads),
+        "attention",
+        position,
+        [tokens, gain_one, weight_rows, out_weight],
+        [
+            like((3, images, rows, local), b16),
+            like((images, rows, LANES), f32),
+            like((padded, local), b16),
+            like((padded, width), b16),
+        ],
+        [pltpu.VMEM((padded, local), f32)],
+        {0: image_block},
+        flops=2 * images * rows * (4 * local * width + 8 * rows * local),
+    )
+    arrived = lax.all_to_all(part.reshape(tensors, chunk, width), "tensor", 0, 0, tiled=True)
+
+    expert_in, expert_out = after((expert_in, expert_out), part)
+    in_rows = lax.dynamic_slice_in_dim(expert_in[0], my_core * half, half, axis=1).T
+    out_rows = lax.dynamic_slice_in_dim(expert_out[0], my_core * half, half, axis=0)
+    mine = jnp.stack([in_rows, out_rows])
+    first, second = mine[:, :quarter], mine[:, quarter:]
+    first_x = cross(first, 1)
+    second_y = cross(second, 2)
+    pair_y = cross(jnp.stack([first, first_x]), 2)
+    pair_x = cross(jnp.stack([second, second_y]), 1)
+
+    member = (expert_ids[..., None] == jnp.arange(experts)).astype(f32)
+    kept = jnp.sum(member * (slot_rank >= 0).astype(f32)[..., None], axis=2)
+    kept = jnp.pad(
+        kept.reshape(token_rows, experts).astype(b16),
+        ((0, padded - token_rows), (0, LANES - experts)),
+    )
+    counts = jnp.pad(
+        jnp.sum(member, axis=(0, 1, 2)) / tensors, (0, width - experts)
+    )[None]
+    x_chunk, payload = kernel_call(
+        functools.partial(chunk_kernel, seq_len),
+        "chunk",
+        position,
+        [tokens, cotangent, kept],
+        [like((chunk, width), b16), like((chunk, width + LANES), b16)],
+        [pltpu.VMEM((flat_rows, width), f32)],
+        {0: image_block, 1: image_block},
+    )
+    payload_mine = lax.all_gather(payload, "expert", axis=0, tiled=True)
+    payload_other = swap_core(payload_mine)
+
+    residual, routed, prob = kernel_call(
+        functools.partial(route_kernel, experts),
+        "route",
+        position,
+        [arrived, x_chunk, gain_two, router_rows],
+        [like((chunk, width), f32), like((chunk, width), b16), like((chunk, LANES), f32)],
+    )
+    blocks = [routed] + [ring(routed, k) for k in range(1, owners)]
+    other_blocks = [swap_core(b) for b in blocks]
+
+    weights = (mine, first_x, second_y, pair_y, pair_x)
+    hidden_b, pre_b, rows_b, row_grad_b, gated_b, back_b = expert_pass(
+        position, other_blocks, payload_other, router_rows, weights, experts
+    )
+    back_other, gated_other = swap_core(back_b), swap_core(gated_b)
+    hidden_a, pre_a, rows_a, row_grad_a, gated_a, back_a = expert_pass(
+        position, blocks, payload_mine, router_rows, weights, experts
+    )
+    joined = kernel_call(
+        join_kernel,
+        "join",
+        position,
+        [back_a, back_other, gated_a, gated_other],
+        [like((chunk, width + 2 * LANES), b16)] * owners + [like((chunk, width), b16)] * owners,
+    )
+    backs = [joined[0]] + [ring(joined[k], -k) for k in range(1, owners)]
+
+    (rows_a, rows_b), _ = lax.optimization_barrier(((rows_a, rows_b), joined[:owners]))
+    own_grad, near_grad, pair_y_grad, pair_x_grad = expert_grads(
+        position,
+        (rows_a, rows_b),
+        (pre_a, pre_b),
+        (hidden_a, hidden_b),
+        (row_grad_a, row_grad_b),
+    )
+    from_y = cross(pair_y_grad, 2)
+    from_x = cross(pair_x_grad, 1)
+    up_first = (near_grad[0].astype(f32) + from_y[1].astype(f32)).astype(b16)
+    up_second = (near_grad[1].astype(f32) + from_x[1].astype(f32)).astype(b16)
+    last_x = cross(up_first, 1)
+    last_y = cross(up_second, 2)
+    grad_first = own_grad[0].astype(f32) + from_y[0].astype(f32) + last_x.astype(f32)
+    grad_second = own_grad[1].astype(f32) + from_x[0].astype(f32) + last_y.astype(f32)
+    grad_half = jnp.concatenate([grad_first, grad_second], axis=1).astype(b16)
+    grad_expert_in, grad_expert_out = kernel_call(
+        weight_out_kernel,
+        "weight_out",
+        position,
+        [grad_half, swap_core(grad_half)],
+        [like((1, width, 2 * half), f32), like((1, 2 * half, width), f32)],
+    )
+
+    residual_grad, attn_grad, small = kernel_call(
+        functools.partial(route_back_kernel, experts, token_rows, owners),
+        "route_back",
+        position,
+        [*backs, prob, residual, payload, router_rows, gain_two, counts],
+        [like((chunk, width), f32), like((chunk, width), b16), like((SMALL, width), f32)],
+    )
+    attn_grad = lax.all_gather(attn_grad, "tensor", axis=0, tiled=True)
+
+    gated_back = after(joined[owners:], attn_grad)
+    combined = residual + gated_back[0].astype(f32)
+    for k in range(1, owners):
+        combined = combined + ring(gated_back[k], -k).astype(f32)
+    combined = combined.astype(b16)
+    block_out = kernel_call(
+        functools.partial(gather_images_kernel, seq_len),
+        "block_out",
+        position,
+        [combined] + [cross(combined, j) for j in range(1, tensors)],
+        [like(tokens.shape, b16)],
+        [pltpu.VMEM((padded, width), f32)],
+    )[0]
+
+    piece = 4 * local // (2 * owners)
+    keep, send, part_grad = kernel_call(
+        functools.partial(attention_back_kernel, seq_len, heads, owners),
+        "attention_back",
+        position,
+        [tokens, gain_one, weight_rows, out_weight, qkv, lse, attended, attn_grad, small],
+        [
+            like((owners, piece, width), f32),
+            like((owners, piece, width), b16),
+            like((tensors, chunk + 2 * SMALL, width), b16),
+        ],
+        [
+            pltpu.VMEM((flat_rows, local), f32),
+            pltpu.VMEM((flat_rows, width), f32),
+            pltpu.VMEM((4 * local, width), f32),
+        ],
+        {0: image_block},
+        flops=2 * images * rows * (8 * local * width + 20 * rows * local),
+    )
+    got = lax.all_to_all(part_grad, "tensor", 0, 0, tiled=True)
+    own_piece, *pieces = kernel_call(
+        add_core_kernel,
+        "add_core",
+        position,
+        [keep, swap_core(send)],
+        [like((piece, width), f32)] + [like((piece, width), b16)] * (owners - 1),
+    )
+    reduced = [ring(p, k + 1) for k, p in enumerate(pieces)]
+    grad_chunk, small = kernel_call(
+        norm_back_kernel,
+        "norm_back",
+        position,
+        [got, x_chunk, residual_grad, gain_one],
+        [like((chunk, width), b16), like((SMALL, width), f32)],
+    )
+    summed = kernel_call(
+        sum_owner_kernel,
+        "sum_owner",
+        position,
+        [own_piece, *reduced, small],
+        [like((piece + 2 * SMALL, width), b16)],
+    )[0]
+    around = [summed] + [ring(summed, k) for k in range(1, owners)]
+    grad_rows = lax.all_gather(grad_chunk, "tensor", axis=0, tiled=True)
+    grad_tokens = kernel_call(
+        functools.partial(images_kernel, seq_len),
+        "grad_tokens",
+        position,
+        [grad_rows],
+        [like(tokens.shape, f32)],
+        [pltpu.VMEM((padded, width), f32)],
+    )[0]
+    token_total = token_rows * cores * owners
+    grad_qkv, grad_out, small, loss = kernel_call(
+        functools.partial(spread_kernel, owners, experts, token_total),
+        "spread",
+        position,
+        around + [swap_core(a) for a in around],
+        [
+            like((3 * local, width), f32),
+            like((local, width), f32),
+            like((SMALL, width), f32),
+            like((SMALL, LANES), f32),
+        ],
+        [
+            pltpu.VMEM((4 * local, width), f32),
+            pltpu.VMEM((2 * owners, SMALL, width), f32),
+        ],
+    )
+    return (
+        block_out,
+        grad_tokens,
+        grad_qkv.reshape(3, local, width).transpose(0, 2, 1),
+        grad_out,
+        small[:experts].T,
+        grad_expert_in,
+        grad_expert_out,
+        small[SMALL - 1],
+        small[experts],
+        loss[0, 0],
+    )
+
+
 def solution(mesh):
     placed = (
         P(("dp", "expert"), None, None),
@@ -268,8 +1039,10 @@
         P(),
         P(),
     )
+    shape = mesh.shape
+    dense = shape["dp"] == 2 and shape["expert"] == 4 and shape["tensor"] == 4
     return jax.shard_map(
-        body,
+        dense_body if dense else body,
         mesh=mesh,
         in_specs=placed,
         out_specs=(

time: 872 us -> 315 us (0.36); the launches traced: 862 us -> 314 us
  blocking collectives: 362 us -> 27.5 us
  waiting for transfers between devices: 202 us -> 79.8 us
  local copies, waits for them, and re-layouts: 139 us -> 17.2 us
  Pallas kernels: 0 us -> 110 us
  matrix products: 74 us -> 0 us
  other arithmetic: 54.2 us -> 11.7 us
  starting transfers between devices: 13 us -> 53.4 us
    unnamed x1 -> x0, blocking collectives: 315 us -> none
    psum x4 -> x0, waiting for transfers between devices: 133 us -> none  [the longest x1 66.8 us: body(): residual = inputs + lax.psum(attn_part, 'tensor')]
    pallas_call x0 -> x16, Pallas kernels: none -> 110 us  [the longest x13 56.2 us: kernel_call(): pl.pallas_call(kernel, grid_spec=pltpu.PrefetchScalarGridSpec(num_scalar_...]
    ppermute x0 -> x39, waiting for transfers between devices: none -> 76.5 us  [the longest x15 56.9 us: ring(): lax.ppermute(value, 'expert', [(i, (i + shift) % size) for i in range(siz...]
    dot_general x20 -> x0, matrix products: 71.3 us -> none  [the longest x1 13.6 us: body(): jnp.einsum('sjcd,jfd->sjcf', grad_arrived, expert_out, preferred_element_...]
    ppermute x0 -> x39, starting transfers between devices: none -> 46.3 us  [the longest x15 24.7 us: ring(): lax.ppermute(value, 'expert', [(i, (i + shift) % size) for i in range(siz...]
    all_to_all x3 -> x2, waiting for transfers between devices: 42.3 us -> 3.33 us  [the longest x1 3.33 us: dense_body(): lax.all_to_all(part.reshape(tensors, chunk, width), 'tensor', 0, 0, tiled...]
    reshape x19 -> x0, local copies, waits for them, and re-layouts: 37.8 us -> none  [the longest x2 9.53 us: body(): lax.all_gather(buffer_back, 'tensor', axis=2, tiled=True)]
  transfers between devices with their start and end apart: 9 -> 42, of which waited for: 7 -> 14; matrix products, arithmetic and copies ran while one was open for 22% -> 5% of each run, Pallas kernels for 0% -> 20%
where the time goes in v1:
time: 315 us; the launch traced here: 314 us
  Pallas kernels  110 us (35%)
  waiting for transfers between devices  79.8 us (25%)
  starting transfers between devices  53.4 us (17%)
  blocking collectives  27.5 us (9%)
  local copies, waits for them, and re-layouts  17.2 us (5%)
  between operations  14.5 us (5%)
  other arithmetic  11.7 us (4%)
    ppermute x15, waiting for transfers between devices, ring(): lax.ppermute(value, 'expert', [(i, (i + shift) % size) for i in range(siz...  56.9 us
    pallas_call x13, Pallas kernels, kernel_call(): pl.pallas_call(kernel, grid_spec=pltpu.PrefetchScalarGridSpec(num_scalar_...  56.2 us
    pallas_call x2, Pallas kernels, expert_pass(): pl.pallas_call(functools.partial(expert_kernel, experts, owners), grid_sp...  39.4 us
    ppermute x15, starting transfers between devices, ring(): lax.ppermute(value, 'expert', [(i, (i + shift) % size) for i in range(siz...  24.7 us
    ppermute x11, starting transfers between devices, cross(): return lax.ppermute(value, 'tensor', [(i, i ^ bit) for i in range(size)])  19.8 us
    ppermute x11, waiting for transfers between devices, cross(): return lax.ppermute(value, 'tensor', [(i, i ^ bit) for i in range(size)])  18.3 us
    all_gather x1, blocking collectives, dense_body(): grad_rows = lax.all_gather(grad_chunk, 'tensor', axis=0, tiled=True)  14.6 us
    pallas_call x1, Pallas kernels, expert_grads(): pl.pallas_call(expert_grad_kernel, grid_spec=pltpu.PrefetchScalarGridSpec...  14.5 us
  transfers between devices with their start and end apart: 42, of which 14 were waited for; matrix products, arithmetic and copies ran while one was open for 5% of the time, Pallas kernels for 20%

profile of v1, /device:TPU:0, one launch (start us, length us, event | category | flops | bytes accessed | tf_op | source)
XLA Modules:
  0.0 314.3 jit_solution(8989666840252409436)
XLA Ops:
  10.4 3.3 %chunk.1 = (bf16[160,768]{1,0:T(8,128)(2,1)}, bf16[160,896]{1,0:T(8,128)(2,1)}) custom-call(s32[3]{0:T(128)} %pad_add_fusion.pos_ref.refs_0_, bf16[3,197,768]{2,1,0:T(8,128)(2,1)} %tok_ref.5, bf16[3,197,768]{2,1,0:T(8,128)(2,1)} %cot_ref.1, bf16[640,128]{1,0:T(8,128)(2,1)} %pad.12.kept_ref), custom_call_target="tpu_custom_call" | custom-call | bytes 2511872 | tf_op jit(solution)/shard_map/chunk/pallas_call | solution.py:285
  14.3 6.9 %attention.1 = (bf16[3,3,208,192]{3,2,1,0:T(8,128)(2,1)}, f32[3,208,128]{2,1,0:T(8,128)}, bf16[640,192]{1,0:T(8,128)(2,1)}, bf16[640,768]{1,0:T(8,128)(2,1)}) custom-call(s32[3]{0:T(128)} %pad_add_fusion.pos_ref.refs_0_, bf16[3,197,768]{2,1,0:T(8,128)(2,1)} %tok_ref.5, f32[1,768]{1,0:T(1,128)} %broadcast_in_dim.12.gain_ref, bf16[576,768]{1,0:T(8,128)(2,1)} %bitcast.44, ...), custom_call_target="tpu_custom_call" | custom-call | flops 1134821376 | bytes 4357632 | tf_op jit(solution)/shard_map/attention/pallas_call | solution.py:285
  27.2 3.5 %all-to-all-start = ((bf16[4,160,768]{2,1,0:T(8,128)(2,1)}), bf16[4,160,768]{2,1,0:T(8,128)(2,1)S(1)}, u32[]{:S(2)}, u32[]{:S(2)}) async-start(bf16[4,160,768]{2,1,0:T(8,128)(2,1)} %bitcast.41), calls=%async_computation | async-start | bytes 1966080 | tf_op jit(solution)/shard_map/all_to_all | solution.py:837
  30.7 10.0 %collective-permute-done.4.refs_9_ = bf16[2,192,768]{2,1,0:T(8,128)(2,1)} collective-permute-done((bf16[2,192,768]{2,1,0:T(8,128)(2,1)S(1)}, bf16[2,192,768]{2,1,0:T(8,128)(2,1)}, u32[]{:S(2)}, u32[]{:S(2)}) %collective-permute-start.4) | collective-permute-done | bytes 589856 | tf_op jit(solution)/shard_map/ppermute | solution.py:778
  49.2 3.3 %all-to-all-done.got_ref = bf16[4,160,768]{2,1,0:T(8,128)(2,1)S(1)} async-done(((bf16[4,160,768]{2,1,0:T(8,128)(2,1)}), bf16[4,160,768]{2,1,0:T(8,128)(2,1)S(1)}, u32[]{:S(2)}, u32[]{:S(2)}) %all-to-all-start) | async-done | bytes 983072 | tf_op jit(solution)/shard_map/all_to_all | solution.py:837
  53.5 3.3 %route.1 = (f32[160,768]{1,0:T(8,128)}, bf16[160,768]{1,0:T(8,128)(2,1)}, f32[160,128]{1,0:T(8,128)}) custom-call(s32[3]{0:T(128)} %pad_add_fusion.pos_ref.refs_0_, bf16[4,160,768]{2,1,0:T(8,128)(2,1)} %copy-done.4, bf16[160,768]{1,0:T(8,128)(2,1)} %get-tuple-element.70.x_ref, f32[1,768]{1,0:T(1,128)} %broadcast_in_dim.13.gain_ref.refs_8_, ...), custom_call_target="tpu_custom_call" | custom-call | bytes 2247680 | tf_op jit(solution)/shard_map/route/pallas_call | solution.py:285
  56.8 3.6 %collective-permute-start.2 = (bf16[160,768]{1,0:T(8,128)(2,1)}, bf16[160,768]{1,0:T(8,128)(2,1)S(1)}, u32[]{:S(2)}, u32[]{:S(2)}) collective-permute-start(bf16[160,768]{1,0:T(8,128)(2,1)} %get-tuple-element.72.refs_1_), channel_id=1, source_target_pairs={{0,12},{4,0},{8,4},{12,8},{1,13},{5,1},{9,5},{13,9},{2,14},{6,2},{... | collective-permute-start | bytes 737288 | tf_op jit(solution)/shard_map/ppermute | solution.py:773
  60.4 6.8 %collective-permute-done.2.refs_4_ = bf16[160,768]{1,0:T(8,128)(2,1)S(1)} collective-permute-done((bf16[160,768]{1,0:T(8,128)(2,1)}, bf16[160,768]{1,0:T(8,128)(2,1)S(1)}, u32[]{:S(2)}, u32[]{:S(2)}) %collective-permute-start.2) | collective-permute-done | bytes 245792 | tf_op jit(solution)/shard_map/ppermute | solution.py:773
  67.2 5.9 %collective-permute-start.1 = (bf16[160,768]{1,0:T(8,128)(2,1)}, bf16[160,768]{1,0:T(8,128)(2,1)S(1)}, u32[]{:S(2)}, u32[]{:S(2)}) collective-permute-start(bf16[160,768]{1,0:T(8,128)(2,1)} %get-tuple-element.72.refs_1_), channel_id=1, source_target_pairs={{0,8},{4,12},{8,0},{12,4},{1,9},{5,13},{9,1},{13,5},{2,10},{6,14},... | collective-permute-start | bytes 737288 | tf_op jit(solution)/shard_map/ppermute | solution.py:773
  73.1 4.4 %collective-permute-done.1.refs_3_ = bf16[160,768]{1,0:T(8,128)(2,1)S(1)} collective-permute-done((bf16[160,768]{1,0:T(8,128)(2,1)}, bf16[160,768]{1,0:T(8,128)(2,1)S(1)}, u32[]{:S(2)}, u32[]{:S(2)}) %collective-permute-start.1) | collective-permute-done | bytes 245792 | tf_op jit(solution)/shard_map/ppermute | solution.py:773
  81.2 19.7 %experts.3 = (bf16[640,1536]{1,0:T(8,128)(2,1)}, bf16[640,1536]{1,0:T(8,128)(2,1)}, bf16[640,768]{1,0:T(8,128)(2,1)}, bf16[640,768]{1,0:T(8,128)(2,1)}, bf16[640,768]{1,0:T(8,128)(2,1)}, /*index=5*/f32[640,896]{1,0:T(8,128)}) custom-call(s32[3]{0:T(128)} %pad_add_fusion.pos_ref.refs_0_, bf16[160,768]{1,0:T(8,128)(2,1)} %copy-done.36, ...), custom_call_target="tpu_custom_call" | custom-call | flops 6039797760 | bytes 14548992 | tf_op jit(solution)/shard_map/experts/pallas_call | solution.py:492
  101.5 19.7 %experts.2 = (bf16[640,1536]{1,0:T(8,128)(2,1)}, bf16[640,1536]{1,0:T(8,128)(2,1)}, bf16[640,768]{1,0:T(8,128)(2,1)}, bf16[640,768]{1,0:T(8,128)(2,1)}, bf16[640,768]{1,0:T(8,128)(2,1)}, /*index=5*/f32[640,896]{1,0:T(8,128)}) custom-call(s32[3]{0:T(128)} %pad_add_fusion.pos_ref.refs_0_, bf16[160,768]{1,0:T(8,128)(2,1)} %get-tuple-element.72.refs_1_, ...), custom_call_target="tpu_custom_call" | custom-call | flops 6039797760 | bytes 14548992 | tf_op jit(solution)/shard_map/experts/pallas_call | solution.py:492
  122.9 5.0 %join.1 = (bf16[160,1024]{1,0:T(8,128)(2,1)}, bf16[160,1024]{1,0:T(8,128)(2,1)}, bf16[160,1024]{1,0:T(8,128)(2,1)}, bf16[160,1024]{1,0:T(8,128)(2,1)}, bf16[160,...) custom-call(s32[3]{0:T(128)} %pad_add_fusion.pos_ref.refs_0_, ...), custom_call_target="tpu_custom_call" | custom-call | bytes 8847360 | tf_op jit(solution)/shard_map/join/pallas_call | solution.py:285
  127.9 14.5 %expert_grads.1 = (bf16[2,2,192,768]{3,2,1,0:T(8,128)(2,1)}, bf16[2,2,192,768]{3,2,1,0:T(8,128)(2,1)}, bf16[2,2,192,768]{3,2,1,0:T(8,128)(2,1)}, bf16[2,2,192,768]{3,2,1,0:T(8,128)(2,1)}) custom-call(s32[3]{0:T(128)} %pad_add_fusion.pos_ref.refs_0_, bf16[640,768]{1,0:T(8,128)(2,1)} %get-tuple-element.113.xa, bf16[640,768]{1,0:T(8,128)(2,1)} %get-tuple-element.114.xb, ...), custom_call_target="tpu_custom_call" | custom-call | flops 6039797760 | bytes 16515072 | tf_op jit(solution)/shard_map/expert_grads/pallas_call | solution.py:554
  142.9 3.6 %collective-permute-start.36 = (bf16[2,2,192,768]{3,2,1,0:T(8,128)(2,1)}, bf16[2,2,192,768]{3,2,1,0:T(8,128)(2,1)S(1)}, u32[]{:S(2)}, u32[]{:S(2)}) collective-permute-start(bf16[2,2,192,768]{3,2,1,0:T(8,128)(2,1)} %get-tuple-element.124), channel_id=1, source_target_pairs={{0,1},{1,0},{2,3},{3,2},{4,5},{5,4},{6,7},{7,6},{8,9},{9,8},{10,11... | collective-permute-start | bytes 3538952 | tf_op jit(solution)/shard_map/ppermute | solution.py:778
  146.5 4.8 %collective-permute-start.14 = (bf16[160,1024]{1,0:T(8,128)(2,1)S(1)}, bf16[160,1024]{1,0:T(8,128)(2,1)S(1)}, u32[]{:S(2)}, u32[]{:S(2)}) collective-permute-start(bf16[160,1024]{1,0:T(8,128)(2,1)S(1)} %copy-done.32), channel_id=1, source_target_pairs={{0,12},{4,0},{8,4},{12,8},{1,13},{5,1},{9,5},{13,9},{2,14},{6,2},{... | collective-permute-start | bytes 983048 | tf_op jit(solution)/shard_map/ppermute | solution.py:773
  152.5 6.9 %collective-permute-done.14.refs_1_ = bf16[160,1024]{1,0:T(8,128)(2,1)S(1)} collective-permute-done((bf16[160,1024]{1,0:T(8,128)(2,1)S(1)}, bf16[160,1024]{1,0:T(8,128)(2,1)S(1)}, u32[]{:S(2)}, u32[]{:S(2)}) %collective-permute-start.14) | collective-permute-done | bytes 327712 | tf_op jit(solution)/shard_map/ppermute | solution.py:773
  159.4 19.5 %collective-permute-done.15.refs_2_ = bf16[160,1024]{1,0:T(8,128)(2,1)S(1)} collective-permute-done((bf16[160,1024]{1,0:T(8,128)(2,1)S(1)}, bf16[160,1024]{1,0:T(8,128)(2,1)S(1)}, u32[]{:S(2)}, u32[]{:S(2)}) %collective-permute-start.15) | collective-permute-done | bytes 327712 | tf_op jit(solution)/shard_map/ppermute | solution.py:773
  179.8 3.7 %route_back.1 = (f32[160,768]{1,0:T(8,128)}, bf16[160,768]{1,0:T(8,128)(2,1)}, f32[8,768]{1,0:T(8,128)}) custom-call(s32[3]{0:T(128)} %pad_add_fusion.pos_ref.refs_0_, bf16[160,1024]{1,0:T(8,128)(2,1)} %get-tuple-element.84.refs_0_, bf16[160,1024]{1,0:T(8,128)(2,1)} %copy-done.12, bf16[160,1024]{1,0:T(8,128)(2,1)} %copy-done.13, ...), custom_call_target="tpu_custom_call" | custom-call | bytes 3135488 | tf_op jit(solution)/shard_map/route_back/pallas_call | solution.py:285
  183.6 12.9 %all_gather.10.up_ref = bf16[640,768]{1,0:T(8,128)(2,1)} all-gather(bf16[160,768]{1,0:T(8,128)(2,1)} %get-tuple-element.89), channel_id=1, replica_groups=mesh['dp'=2,'expert'=4,'tensor'=4] {'tensor'}, dimensions={0}, use_global_device_ids=true | all-gather | bytes 1228800 | tf_op jit(solution)/shard_map/all_gather | solution.py:929
  196.4 10.1 %attention_back.1 = (f32[4,96,768]{2,1,0:T(8,128)}, bf16[4,96,768]{2,1,0:T(8,128)(2,1)}, bf16[4,176,768]{2,1,0:T(8,128)(2,1)}) custom-call(s32[3]{0:T(128)} %pad_add_fusion.pos_ref.refs_0_, bf16[3,197,768]{2,1,0:T(8,128)(2,1)} %tok_ref.5, f32[1,768]{1,0:T(1,128)} %broadcast_in_dim.12.gain_ref, bf16[576,768]{1,0:T(8,128)(2,1)} %bitcast.45, ...), custom_call_target="tpu_custom_call" | custom-call | flops 2469003264 | bytes 7233024 | tf_op jit(solution)/shard_map/attention_back/pallas_call | solution.py:285
  209.9 3.5 %all-to-all-start.1 = ((bf16[4,176,768]{2,1,0:T(8,128)(2,1)}), bf16[4,176,768]{2,1,0:T(8,128)(2,1)S(1)}, u32[]{:S(2)}, u32[]{:S(2)}) async-start(bf16[4,176,768]{2,1,0:T(8,128)(2,1)} %get-tuple-element.98), calls=%async_computation.1 | async-start | bytes 2162688 | tf_op jit(solution)/shard_map/all_to_all | solution.py:964
  225.3 5.4 %collective-permute-done.37 = bf16[2,192,768]{2,1,0:T(8,128)(2,1)} collective-permute-done((bf16[2,192,768]{2,1,0:T(8,128)(2,1)}, bf16[2,192,768]{2,1,0:T(8,128)(2,1)}, u32[]{:S(2)}, u32[]{:S(2)}) %collective-permute-start.37) | collective-permute-done | bytes 589856 | tf_op jit(solution)/shard_map/ppermute | solution.py:778
  232.6 9.0 %collective-permute-done.18 = bf16[160,768]{1,0:T(8,128)(2,1)S(1)} collective-permute-done((bf16[160,768]{1,0:T(8,128)(2,1)}, bf16[160,768]{1,0:T(8,128)(2,1)S(1)}, u32[]{:S(2)}, u32[]{:S(2)}) %collective-permute-start.18) | collective-permute-done | bytes 245792 | tf_op jit(solution)/shard_map/ppermute | solution.py:773
  244.1 4.6 %collective-permute-start.21 = (bf16[160,768]{1,0:T(8,128)(2,1)}, bf16[160,768]{1,0:T(8,128)(2,1)}, u32[]{:S(2)}, u32[]{:S(2)}) collective-permute-start(bf16[160,768]{1,0:T(8,128)(2,1)} %add_convert_fusion.2.refs_0_), channel_id=1, source_target_pairs={{0,2},{1,3},{2,0},{3,1},{4,6},{5,7},{6,4},{7,5},{8,10},{9,11},{10,... | collective-permute-start | bytes 737288 | tf_op jit(solution)/shard_map/ppermute | solution.py:778
  248.9 6.1 %collective-permute-done.25.refs_1_ = bf16[96,768]{1,0:T(8,128)(2,1)S(1)} collective-permute-done((bf16[96,768]{1,0:T(8,128)(2,1)S(1)}, bf16[96,768]{1,0:T(8,128)(2,1)S(1)}, u32[]{:S(2)}, u32[]{:S(2)}) %collective-permute-start.25) | collective-permute-done | bytes 147488 | tf_op jit(solution)/shard_map/ppermute | solution.py:773
  262.5 3.8 %collective-permute-start.29 = (bf16[112,768]{1,0:T(8,128)(2,1)}, bf16[112,768]{1,0:T(8,128)(2,1)S(1)}, u32[]{:S(2)}, u32[]{:S(2)}) collective-permute-start(bf16[112,768]{1,0:T(8,128)(2,1)} %sum_owner.1.refs_0_), channel_id=1, source_target_pairs={{0,12},{4,0},{8,4},{12,8},{1,13},{5,1},{9,5},{13,9},{2,14},{6,2},{... | collective-permute-start | bytes 516104 | tf_op jit(solution)/shard_map/ppermute | solution.py:773
  270.0 3.7 %collective-permute-done.28.refs_2_ = bf16[112,768]{1,0:T(8,128)(2,1)S(1)} collective-permute-done((bf16[112,768]{1,0:T(8,128)(2,1)}, bf16[112,768]{1,0:T(8,128)(2,1)S(1)}, u32[]{:S(2)}, u32[]{:S(2)}) %collective-permute-start.28) | collective-permute-done | bytes 172064 | tf_op jit(solution)/shard_map/ppermute | solution.py:773
  274.3 14.6 %all_gather.11.rows_ref = bf16[640,768]{1,0:T(8,128)(2,1)} all-gather(bf16[160,768]{1,0:T(8,128)(2,1)S(1)} %copy-done.16), channel_id=1, replica_groups=mesh['dp'=2,'expert'=4,'tensor'=4] {'tensor'}, dimensions={0}, use_global_device_ids=true | all-gather | bytes 1228800 | tf_op jit(solution)/shard_map/all_gather | solution.py:988
  288.9 3.3 %grad_tokens.1 = f32[3,197,768]{2,1,0:T(8,128)} custom-call(s32[3]{0:T(128)} %pad_add_fusion.pos_ref.refs_0_, bf16[640,768]{1,0:T(8,128)(2,1)} %all_gather.11.rows_ref), custom_call_target="tpu_custom_call" | custom-call | bytes 2798592 | tf_op jit(solution)/shard_map/grad_tokens/pallas_call | solution.py:285
  293.7 3.8 %spread.1 = (f32[576,768]{1,0:T(8,128)}, f32[192,768]{1,0:T(8,128)}, f32[8,768]{1,0:T(8,128)}, f32[8,128]{1,0:T(8,128)}) custom-call(s32[3]{0:T(128)} %pad_add_fusion.pos_ref.refs_0_, bf16[112,768]{1,0:T(8,128)(2,1)} %sum_owner.1.refs_0_, bf16[112,768]{1,0:T(8,128)(2,1)} %copy-done.18, bf16[112,768]{1,0:T(8,128)(2,1)} %copy-done.19, ...), custom_call_target="tpu_custom_call" | custom-call | bytes 3764224 | tf_op jit(solution)/shard_map/spread/pallas_call | solution.py:285
  302.6 4.9 %weight_out.1 = (f32[1,768,768]{2,1,0:T(8,128)}, f32[1,768,768]{2,1,0:T(8,128)}) custom-call(s32[3]{0:T(128)} %pad_add_fusion.pos_ref.refs_0_, bf16[2,384,768]{2,1,0:T(8,128)(2,1)} %copy-done.2, bf16[2,384,768]{2,1,0:T(8,128)(2,1)} %copy-done.8), custom_call_target="tpu_custom_call" | custom-call | bytes 7077888 | tf_op jit(solution)/shard_map/weight_out/pallas_call | solution.py:285
  (180 shorter events, 65.7 us)
Async XLA Ops:
  7.2 40.7 %all-gather.2.cloned.1.call-start = ((), (), s32[]{:S(2)}) async-start(), calls=%async_computation.2 | async-start | bytes 1433600 | tf_op jit(solution)/shard_map/all_gather | solution.py:867
  22.6 18.1 %collective-permute-start.4 = (bf16[2,192,768]{2,1,0:T(8,128)(2,1)S(1)}, bf16[2,192,768]{2,1,0:T(8,128)(2,1)}, u32[]{:S(2)}, u32[]{:S(2)}) collective-permute-start(bf16[2,192,768]{2,1,0:T(8,128)(2,1)S(1)} %get-tuple-element.136), channel_id=1, source_target_pairs={{0,2},{1,3},{2,0},{3,1},{4,6},{5,7},{6,4},{7,5},{8,10},{9,11},{10,... | collective-permute-start | bytes 1769480 | tf_op jit(solution)/shard_map/ppermute | solution.py:778
  25.7 18.5 %collective-permute-start.3 = (bf16[2,192,768]{2,1,0:T(8,128)(2,1)S(1)}, bf16[2,192,768]{2,1,0:T(8,128)(2,1)}, u32[]{:S(2)}, u32[]{:S(2)}) collective-permute-start(bf16[2,192,768]{2,1,0:T(8,128)(2,1)S(1)} %get-tuple-element.137), channel_id=1, source_target_pairs={{0,1},{1,0},{2,3},{3,2},{4,5},{5,4},{6,7},{7,6},{8,9},{9,8},{10,11... | collective-permute-start | bytes 1769480 | tf_op jit(solution)/shard_map/ppermute | solution.py:778
  27.2 25.3 %all-to-all-start = ((bf16[4,160,768]{2,1,0:T(8,128)(2,1)}), bf16[4,160,768]{2,1,0:T(8,128)(2,1)S(1)}, u32[]{:S(2)}, u32[]{:S(2)}) async-start(bf16[4,160,768]{2,1,0:T(8,128)(2,1)} %bitcast.41), calls=%async_computation | async-start | bytes 1966080 | tf_op jit(solution)/shard_map/all_to_all | solution.py:837
  42.9 37.6 %collective-permute-start.6 = (bf16[2,2,192,768]{3,2,1,0:T(8,128)(2,1)}, bf16[2,2,192,768]{3,2,1,0:T(8,128)(2,1)}, u32[]{:S(2)}, u32[]{:S(2)}) collective-permute-start(bf16[2,2,192,768]{3,2,1,0:T(8,128)(2,1)} %pad_maximum_fusion.2), channel_id=1, source_target_pairs={{0,1},{1,0},{2,3},{3,2},{4,5},{5,4},{6,7},{7,6},{8,9},{9,8},{10,11... | collective-permute-start | bytes 3538952 | tf_op jit(solution)/shard_map/ppermute | solution.py:778
  46.4 34.1 %collective-permute-start.5 = (bf16[2,2,192,768]{3,2,1,0:T(8,128)(2,1)}, bf16[2,2,192,768]{3,2,1,0:T(8,128)(2,1)}, u32[]{:S(2)}, u32[]{:S(2)}) collective-permute-start(bf16[2,2,192,768]{3,2,1,0:T(8,128)(2,1)} %pad_maximum_fusion.1), channel_id=1, source_target_pairs={{0,2},{1,3},{2,0},{3,1},{4,6},{5,7},{6,4},{7,5},{8,10},{9,11},{10,... | collective-permute-start | bytes 3538952 | tf_op jit(solution)/shard_map/ppermute | solution.py:778
  47.9 32.5 %collective-permute-start.11 = (bf16[640,896]{1,0:T(8,128)(2,1)}, bf16[640,896]{1,0:T(8,128)(2,1)}, u32[]{:S(2)}, u32[]{:S(2)}) collective-permute-start(bf16[640,896]{1,0:T(8,128)(2,1)} %all-gather.2.cloned.1.call-done.refs_5_), channel_id=1, source_target_pairs={{0,16},{16,0},{1,17},{17,1},{2,18},{18,2},{3,19},{19,3},{4,20},{20... | collective-permute-start | bytes 3440648 | tf_op jit(solution)/shard_map/ppermute | solution.py:768
  60.4 12.6 %collective-permute-start = (bf16[160,768]{1,0:T(8,128)(2,1)}, bf16[160,768]{1,0:T(8,128)(2,1)S(1)}, u32[]{:S(2)}, u32[]{:S(2)}) collective-permute-start(bf16[160,768]{1,0:T(8,128)(2,1)} %get-tuple-element.72.refs_1_), channel_id=1, source_target_pairs={{0,4},{4,8},{8,12},{12,0},{1,5},{5,9},{9,13},{13,1},{2,6},{6,10},{... | collective-permute-start | bytes 737288 | tf_op jit(solution)/shard_map/ppermute | solution.py:773
  100.9 20.3 %collective-permute-start.12 = (f32[640,896]{1,0:T(8,128)}, f32[640,896]{1,0:T(8,128)S(1)}, u32[]{:S(2)}, u32[]{:S(2)}) collective-permute-start(f32[640,896]{1,0:T(8,128)} %get-tuple-element.77), channel_id=1, source_target_pairs={{0,16},{16,0},{1,17},{17,1},{2,18},{18,2},{3,19},{19,3},{4,20},{20... | collective-permute-start | bytes 6881288 | tf_op jit(solution)/shard_map/ppermute | solution.py:768
  101.2 20.0 %collective-permute-start.13 = (bf16[640,768]{1,0:T(8,128)(2,1)}, bf16[640,768]{1,0:T(8,128)(2,1)S(1)}, u32[]{:S(2)}, u32[]{:S(2)}) collective-permute-start(bf16[640,768]{1,0:T(8,128)(2,1)} %get-tuple-element.79), channel_id=1, source_target_pairs={{0,16},{16,0},{1,17},{17,1},{2,18},{18,2},{3,19},{19,3},{4,20},{20... | collective-permute-start | bytes 2949128 | tf_op jit(solution)/shard_map/ppermute | solution.py:768
  142.4 64.2 %collective-permute-start.34 = (bf16[2,2,192,768]{3,2,1,0:T(8,128)(2,1)}, bf16[2,2,192,768]{3,2,1,0:T(8,128)(2,1)S(1)}, u32[]{:S(2)}, u32[]{:S(2)}) collective-permute-start(bf16[2,2,192,768]{3,2,1,0:T(8,128)(2,1)} %get-tuple-element.122), channel_id=1, source_target_pairs={{0,2},{1,3},{2,0},{3,1},{4,6},{5,7},{6,4},{7,5},{8,10},{9,11},{10,... | collective-permute-start | bytes 3538952 | tf_op jit(solution)/shard_map/ppermute | solution.py:778
  142.9 63.7 %collective-permute-start.36 = (bf16[2,2,192,768]{3,2,1,0:T(8,128)(2,1)}, bf16[2,2,192,768]{3,2,1,0:T(8,128)(2,1)S(1)}, u32[]{:S(2)}, u32[]{:S(2)}) collective-permute-start(bf16[2,2,192,768]{3,2,1,0:T(8,128)(2,1)} %get-tuple-element.124), channel_id=1, source_target_pairs={{0,1},{1,0},{2,3},{3,2},{4,5},{5,4},{6,7},{7,6},{8,9},{9,8},{10,11... | collective-permute-start | bytes 3538952 | tf_op jit(solution)/shard_map/ppermute | solution.py:778
  146.5 12.9 %collective-permute-start.14 = (bf16[160,1024]{1,0:T(8,128)(2,1)S(1)}, bf16[160,1024]{1,0:T(8,128)(2,1)S(1)}, u32[]{:S(2)}, u32[]{:S(2)}) collective-permute-start(bf16[160,1024]{1,0:T(8,128)(2,1)S(1)} %copy-done.32), channel_id=1, source_target_pairs={{0,12},{4,0},{8,4},{12,8},{1,13},{5,1},{9,5},{13,9},{2,14},{6,2},{... | collective-permute-start | bytes 983048 | tf_op jit(solution)/shard_map/ppermute | solution.py:773
  151.3 27.7 %collective-permute-start.15 = (bf16[160,1024]{1,0:T(8,128)(2,1)S(1)}, bf16[160,1024]{1,0:T(8,128)(2,1)S(1)}, u32[]{:S(2)}, u32[]{:S(2)}) collective-permute-start(bf16[160,1024]{1,0:T(8,128)(2,1)S(1)} %copy-done.31), channel_id=1, source_target_pairs={{0,8},{4,12},{8,0},{12,4},{1,9},{5,13},{9,1},{13,5},{2,10},{6,14},... | collective-permute-start | bytes 983048 | tf_op jit(solution)/shard_map/ppermute | solution.py:773
  151.3 27.7 %collective-permute-start.16 = (bf16[160,1024]{1,0:T(8,128)(2,1)S(1)}, bf16[160,1024]{1,0:T(8,128)(2,1)S(1)}, u32[]{:S(2)}, u32[]{:S(2)}) collective-permute-start(bf16[160,1024]{1,0:T(8,128)(2,1)S(1)} %copy-done.30), channel_id=1, source_target_pairs={{0,4},{4,8},{8,12},{12,0},{1,5},{5,9},{9,13},{13,1},{2,6},{6,10},{... | collective-permute-start | bytes 983048 | tf_op jit(solution)/shard_map/ppermute | solution.py:773
  207.9 16.4 %collective-permute-start.35 = (bf16[2,192,768]{2,1,0:T(8,128)(2,1)}, bf16[2,192,768]{2,1,0:T(8,128)(2,1)}, u32[]{:S(2)}, u32[]{:S(2)}) collective-permute-start(bf16[2,192,768]{2,1,0:T(8,128)(2,1)} %get-tuple-element.134), channel_id=1, source_target_pairs={{0,1},{1,0},{2,3},{3,2},{4,5},{5,4},{6,7},{7,6},{8,9},{9,8},{10,11... | collective-permute-start | bytes 1769480 | tf_op jit(solution)/shard_map/ppermute | solution.py:778
  208.4 22.3 %collective-permute-start.37 = (bf16[2,192,768]{2,1,0:T(8,128)(2,1)}, bf16[2,192,768]{2,1,0:T(8,128)(2,1)}, u32[]{:S(2)}, u32[]{:S(2)}) collective-permute-start(bf16[2,192,768]{2,1,0:T(8,128)(2,1)} %get-tuple-element.135), channel_id=1, source_target_pairs={{0,2},{1,3},{2,0},{3,1},{4,6},{5,7},{6,4},{7,5},{8,10},{9,11},{10,... | collective-permute-start | bytes 1769480 | tf_op jit(solution)/shard_map/ppermute | solution.py:778
  209.9 45.7 %all-to-all-start.1 = ((bf16[4,176,768]{2,1,0:T(8,128)(2,1)}), bf16[4,176,768]{2,1,0:T(8,128)(2,1)S(1)}, u32[]{:S(2)}, u32[]{:S(2)}) async-start(bf16[4,176,768]{2,1,0:T(8,128)(2,1)} %get-tuple-element.98), calls=%async_computation.1 | async-start | bytes 2162688 | tf_op jit(solution)/shard_map/all_to_all | solution.py:964
  213.4 19.1 %collective-permute-start.17 = (bf16[160,768]{1,0:T(8,128)(2,1)}, bf16[160,768]{1,0:T(8,128)(2,1)S(1)}, u32[]{:S(2)}, u32[]{:S(2)}) collective-permute-start(bf16[160,768]{1,0:T(8,128)(2,1)} %get-tuple-element.91), channel_id=1, source_target_pairs={{0,12},{4,0},{8,4},{12,8},{1,13},{5,1},{9,5},{13,9},{2,14},{6,2},{... | collective-permute-start | bytes 737288 | tf_op jit(solution)/shard_map/ppermute | solution.py:773
  213.5 28.1 %collective-permute-start.18 = (bf16[160,768]{1,0:T(8,128)(2,1)}, bf16[160,768]{1,0:T(8,128)(2,1)S(1)}, u32[]{:S(2)}, u32[]{:S(2)}) collective-permute-start(bf16[160,768]{1,0:T(8,128)(2,1)} %get-tuple-element.92), channel_id=1, source_target_pairs={{0,8},{4,12},{8,0},{12,4},{1,9},{5,13},{9,1},{13,5},{2,10},{6,14},... | collective-permute-start | bytes 737288 | tf_op jit(solution)/shard_map/ppermute | solution.py:773
  216.5 25.1 %collective-permute-start.19 = (bf16[160,768]{1,0:T(8,128)(2,1)}, bf16[160,768]{1,0:T(8,128)(2,1)S(1)}, u32[]{:S(2)}, u32[]{:S(2)}) collective-permute-start(bf16[160,768]{1,0:T(8,128)(2,1)} %get-tuple-element.93), channel_id=1, source_target_pairs={{0,4},{4,8},{8,12},{12,0},{1,5},{5,9},{9,13},{13,1},{2,6},{6,10},{... | collective-permute-start | bytes 737288 | tf_op jit(solution)/shard_map/ppermute | solution.py:773
  224.3 24.5 %collective-permute-start.24 = (bf16[96,768]{1,0:T(8,128)(2,1)}, bf16[96,768]{1,0:T(8,128)(2,1)S(1)}, u32[]{:S(2)}, u32[]{:S(2)}) collective-permute-start(bf16[96,768]{1,0:T(8,128)(2,1)} %get-tuple-element.104), channel_id=1, source_target_pairs={{0,4},{4,8},{8,12},{12,0},{1,5},{5,9},{9,13},{13,1},{2,6},{6,10},{... | collective-permute-start | bytes 442376 | tf_op jit(solution)/shard_map/ppermute | solution.py:773
  232.5 69.0 %collective-permute-start.38 = (bf16[2,384,768]{2,1,0:T(8,128)(2,1)S(1)}, bf16[2,384,768]{2,1,0:T(8,128)(2,1)S(1)}, u32[]{:S(2)}, u32[]{:S(2)}) collective-permute-start(bf16[2,384,768]{2,1,0:T(8,128)(2,1)S(1)} %pad_maximum_fusion.3.mine_ref), channel_id=1, source_target_pairs={{0,16},{16,0},{1,17},{17,1},{2,18},{18,2},{3,19},{19,3},{4,20},{20... | collective-permute-start | bytes 3538952 | tf_op jit(solution)/shard_map/ppermute | solution.py:768
  242.5 19.9 %collective-permute-start.20 = (bf16[160,768]{1,0:T(8,128)(2,1)}, bf16[160,768]{1,0:T(8,128)(2,1)}, u32[]{:S(2)}, u32[]{:S(2)}) collective-permute-start(bf16[160,768]{1,0:T(8,128)(2,1)} %add_convert_fusion.2.refs_0_), channel_id=1, source_target_pairs={{0,1},{1,0},{2,3},{3,2},{4,5},{5,4},{6,7},{7,6},{8,9},{9,8},{10,11... | collective-permute-start | bytes 737288 | tf_op jit(solution)/shard_map/ppermute | solution.py:778
  244.1 18.4 %collective-permute-start.21 = (bf16[160,768]{1,0:T(8,128)(2,1)}, bf16[160,768]{1,0:T(8,128)(2,1)}, u32[]{:S(2)}, u32[]{:S(2)}) collective-permute-start(bf16[160,768]{1,0:T(8,128)(2,1)} %add_convert_fusion.2.refs_0_), channel_id=1, source_target_pairs={{0,2},{1,3},{2,0},{3,1},{4,6},{5,7},{6,4},{7,5},{8,10},{9,11},{10,... | collective-permute-start | bytes 737288 | tf_op jit(solution)/shard_map/ppermute | solution.py:778
  248.8 11.1 %collective-permute-start.26 = (bf16[96,768]{1,0:T(8,128)(2,1)}, bf16[96,768]{1,0:T(8,128)(2,1)}, u32[]{:S(2)}, u32[]{:S(2)}) collective-permute-start(bf16[96,768]{1,0:T(8,128)(2,1)} %get-tuple-element.106), channel_id=1, source_target_pairs={{0,12},{4,0},{8,4},{12,8},{1,13},{5,1},{9,5},{13,9},{2,14},{6,2},{... | collective-permute-start | bytes 442376 | tf_op jit(solution)/shard_map/ppermute | solution.py:773
  262.4 11.3 %collective-permute-start.28 = (bf16[112,768]{1,0:T(8,128)(2,1)}, bf16[112,768]{1,0:T(8,128)(2,1)S(1)}, u32[]{:S(2)}, u32[]{:S(2)}) collective-permute-start(bf16[112,768]{1,0:T(8,128)(2,1)} %sum_owner.1.refs_0_), channel_id=1, source_target_pairs={{0,8},{4,12},{8,0},{12,4},{1,9},{5,13},{9,1},{13,5},{2,10},{6,14},... | collective-permute-start | bytes 516104 | tf_op jit(solution)/shard_map/ppermute | solution.py:773
  262.5 11.2 %collective-permute-start.29 = (bf16[112,768]{1,0:T(8,128)(2,1)}, bf16[112,768]{1,0:T(8,128)(2,1)S(1)}, u32[]{:S(2)}, u32[]{:S(2)}) collective-permute-start(bf16[112,768]{1,0:T(8,128)(2,1)} %sum_owner.1.refs_0_), channel_id=1, source_target_pairs={{0,12},{4,0},{8,4},{12,8},{1,13},{5,1},{9,5},{13,9},{2,14},{6,2},{... | collective-permute-start | bytes 516104 | tf_op jit(solution)/shard_map/ppermute | solution.py:773
  269.5 22.7 %collective-permute-start.30 = (bf16[112,768]{1,0:T(8,128)(2,1)S(1)}, bf16[112,768]{1,0:T(8,128)(2,1)S(1)}, u32[]{:S(2)}, u32[]{:S(2)}) collective-permute-start(bf16[112,768]{1,0:T(8,128)(2,1)S(1)} %copy-done.11), channel_id=1, source_target_pairs={{0,16},{16,0},{1,17},{17,1},{2,18},{18,2},{3,19},{19,3},{4,20},{20... | collective-permute-start | bytes 516104 | tf_op jit(solution)/shard_map/ppermute | solution.py:768
  270.0 22.2 %collective-permute-start.31 = (bf16[112,768]{1,0:T(8,128)(2,1)S(1)}, bf16[112,768]{1,0:T(8,128)(2,1)S(1)}, u32[]{:S(2)}, u32[]{:S(2)}) collective-permute-start(bf16[112,768]{1,0:T(8,128)(2,1)S(1)} %collective-permute-done.27.refs_1_), channel_id=1, source_target_pairs={{0,16},{16,0},{1,17},{17,1},{2,18},{18,2},{3,19},{19,3},{4,20},{20... | collective-permute-start | bytes 516104 | tf_op jit(solution)/shard_map/ppermute | solution.py:768
  273.7 18.5 %collective-permute-start.32 = (bf16[112,768]{1,0:T(8,128)(2,1)S(1)}, bf16[112,768]{1,0:T(8,128)(2,1)S(1)}, u32[]{:S(2)}, u32[]{:S(2)}) collective-permute-start(bf16[112,768]{1,0:T(8,128)(2,1)S(1)} %collective-permute-done.28.refs_2_), channel_id=1, source_target_pairs={{0,16},{16,0},{1,17},{17,1},{2,18},{18,2},{3,19},{19,3},{4,20},{20... | collective-permute-start | bytes 516104 | tf_op jit(solution)/shard_map/ppermute | solution.py:768
  273.8 18.5 %collective-permute-start.33 = (bf16[112,768]{1,0:T(8,128)(2,1)S(1)}, bf16[112,768]{1,0:T(8,128)(2,1)S(1)}, u32[]{:S(2)}, u32[]{:S(2)}) collective-permute-start(bf16[112,768]{1,0:T(8,128)(2,1)S(1)} %collective-permute-done.29.refs_3_), channel_id=1, source_target_pairs={{0,16},{16,0},{1,17},{17,1},{2,18},{18,2},{3,19},{19,3},{4,20},{20... | collective-permute-start | bytes 516104 | tf_op jit(solution)/shard_map/ppermute | solution.py:768
  (51 other events, 397.8 us)
Sparse Core Ops, SparseCore 0:
  13.9 32.2 all-gather.1
